TPU v7x, 32 devices: a whole 2x2x4 slice. The times are simulated.
32 devices in a mesh: tile: 8 (over z, y), band: 4 (over x, core).
Axes of the slice: x: 2, y: 2, z: 4, core: 2. Of those that a mesh axis runs over, the one named last changes fastest.
Arguments:
- background: float32 [36, 36, 8, 8, 128], P('band', None, 'tile'), may hold values from 0.2 to 2
- tangent: float32 [36, 36, 8, 8, 128], P('band', None, 'tile'), may hold values from -6 to 6
- sea_mask: int32 [8, 8, 128], P('tile'), may hold values 0 or 1
- coupling: float32 [36], P('band'), may hold values from 0.005 to 0.05
- freq_offsets: int32 [2], replicated, may hold values from 1 to 3, as said below
- dir_offsets: int32 [2], replicated, may hold values from 1 to 5
Outputs:
- background_out: float32 [36, 36, 8, 8, 128], P('band', None, 'tile')
- tangent_out: float32 [36, 36, 8, 8, 128], P('band', None, 'tile')
Inputs may be any that keep to these rules, and one draw needn't show every extreme that they name: `freq_offsets`: one of the two offsets equals 3, the other is smaller.
All inputs are finite; a program needn't handle non-finite values. No bound on the sum of `sea_mask` on one device may be relied on, other than what follows from the above.
Results may differ from a plain program's by a relative error of at most 0.00002.
Values sent between devices are 32-bit elements; how exact they have to be, the bound alone decides.
No kernel may reach another device: no remote copies, remote signals or barrier semaphores. Data moves between devices by JAX's collectives and lax.ppermute only.
A program may use at most 64 MiB of HBM per device.

v0:
```python
import functools
import math

import jax
import jax.numpy as jnp
import numpy as np
from jax import lax
from jax.experimental import pallas as pl
from jax.experimental.pallas import tpu as pltpu
from jax.sharding import PartitionSpec as P


TY = 4
FH = 3
STEPS = 2

weight_plus = 1.0 / 1.25**4
weight_minus = 1.0 / 0.75**4
weight_cross = 1.0 / (1.0 - 0.25**2) ** 4
source_step = 0.5

VM = pl.BlockSpec(memory_space=pltpu.VMEM)
SM = pl.BlockSpec(memory_space=pltpu.SMEM)
HBM = pl.BlockSpec(memory_space=pltpu.HBM)
f32 = jnp.float32
STAGES = 2


def rotate(x, shift, axis):
    shift = shift % x.shape[axis]
    return x if shift == 0 else pltpu.roll(x, shift, axis)


class Plan:
    def __init__(self, bins, nd, rows, lanes):
        self.bins, self.nd, self.rows, self.lanes = bins, nd, rows, lanes
        self.half, self.quad = nd // 2, nd // 4
        self.group = lanes // nd
        self.groups = bins // self.group
        assert self.group == FH and bins == FH * self.groups and nd == 4 * self.quad and bins >= 2 * FH
        angles = (np.arange(self.quad) + 0.5) * (2.0 * math.pi / nd)
        self.cosines, self.sines = np.cos(angles), np.sin(angles)
        self.tile = (rows, lanes)
        self.levels = bins + 2 * FH
        self.last = bins * self.quad
        self.weight_tiles = -(-3 * self.quad // rows)
        self.sent_rows = FH * self.quad
        self.sent = 2 * self.sent_rows + 5

    def pair(self, sign, i):
        return (i, self.half - 1 - i) if sign == 0 else (self.nd - 1 - i, self.half + i)

    def tiles(self):
        for sign in range(2):
            for i in range(self.quad):
                for side, j in enumerate(self.pair(sign, i)):
                    for field in range(2):
                        yield sign, i, side, j, field, 4 * (sign * self.quad + i) + 2 * side + field


def iotas(plan):
    sub = lax.broadcasted_iota(jnp.int32, plan.tile, 0)
    lane = lax.broadcasted_iota(jnp.int32, plan.tile, 1)
    return sub, lane


def row_parity():
    return lax.rem(lax.rem(lax.axis_index("tile") + TY // 2, TY), 2)


def band_parity():
    return lax.rem(lax.axis_index("band"), 2)


def level_speed(plan, bands, offset):
    band = lax.axis_index("band")
    speed = jnp.float32(0.7 * 1.1 ** -offset)
    for n in range(1, bands):
        speed = jnp.where(band == n, jnp.float32(0.7 * 1.1 ** -(n * plan.bins + offset)), speed)
    return speed


def lane_weights(plan):
    _, lane = iotas(plan)
    index = lax.rem(lax.rem(lane, plan.nd) // 2, plan.quad)
    cosine = sine = jnp.zeros(plan.tile, f32)
    for i in range(plan.quad):
        cosine = jnp.where(index == i, float(plan.cosines[i]), cosine)
        sine = jnp.where(index == i, float(plan.sines[i]), sine)
    return cosine, sine


def fill_weights(plan, bands, weight_ref):
    sub, _ = iotas(plan)
    for t in range(plan.weight_tiles):
        slope = rest = jnp.zeros(plan.tile, f32)
        for row in range(min(plan.rows, 3 * plan.quad - t * plan.rows)):
            i, c = divmod(t * plan.rows + row, 3)
            cosine, sine = float(plan.cosines[i]), float(plan.sines[i])
            slope = jnp.where(sub == row, (-cosine - sine, cosine, sine)[c], slope)
            rest = jnp.where(sub == row, 1.0 if c == 0 else 0.0, rest)
        for level in range(plan.levels):
            weight_ref[level, t] = rest + level_speed(plan, bands, level - FH) * slope


def spread(row, plan):
    return jnp.broadcast_to(row, plan.tile)


def pack_rows(plan, k, f_ref, g_ref, out_ref):
    sub, _ = iotas(plan)
    for sign in range(2):
        start = plan.rows - 2 if sign == 0 else 0
        for i in range(plan.quad):
            tiles = [ref[k, j] for j in plan.pair(sign, i) for ref in (f_ref, g_ref)]
            edge = rotate(tiles[3], 6 - start, 0)
            for n in (2, 1, 0):
                edge = jnp.where(sub < 2 * n + 2, rotate(tiles[n], 2 * n - start, 0), edge)
            out_ref[sign, k * plan.quad + i] = edge


def send_out(plan, f_ref, g_ref, rows_ref, row_refs, raw_refs):
    parity, band = row_parity(), band_parity()
    for n in range(2):
        towards = parity if n == 0 else 1 - parity
        row_refs[n][...] = rows_ref[towards]
        start = (band if n == 1 else 1 - band) * (plan.bins - FH)
        for field, ref in enumerate((f_ref, g_ref)):
            raw_refs[n][field] = ref[pl.ds(start, FH)]


def load_kernel(plan, bands, f_hbm, g_hbm, mask_ref, f_ref, g_ref, even_ref, odd_ref, raw_even, raw_odd, weight_ref, rows_ref, sems):
    mask = mask_ref[...].astype(f32)
    pairs = ((f_hbm, f_ref), (g_hbm, g_ref))
    copies = [
        [pltpu.make_async_copy(src.at[k], dst.at[k], sems.at[n, k]) for n, (src, dst) in enumerate(pairs)]
        for k in range(plan.bins)
    ]
    for level in copies:
        for copy in level:
            copy.start()
    fill_weights(plan, bands, weight_ref)
    for sign in range(2):
        rows_ref[sign, plan.last] = mask
    for k in range(plan.bins):
        for copy in copies[k]:
            copy.wait()

        def clear(j, _):
            f_ref[k, j] = f_ref[k, j] * mask
            g_ref[k, j] = g_ref[k, j] * mask
            return 0

        lax.fori_loop(0, plan.nd, clear, 0, unroll=12)
    lax.fori_loop(0, plan.bins, lambda k, _: pack_rows(plan, k, f_ref, g_ref, rows_ref) or 0, 0)
    send_out(plan, f_ref, g_ref, rows_ref, (even_ref, odd_ref), (raw_even, raw_odd))


def pack_kernel(plan, f_ref, g_ref, mask_ref, col_ref, even_ref, odd_ref):
    mask = mask_ref[...].astype(f32)
    _, lane = iotas(plan)
    pair_lane = lane // 2
    rows, lanes = plan.tile
    upward = row_parity() == 0
    for side in range(2):
        col_ref[side, 2 * plan.groups] = mask

    def part(at, _):
        packed = [[jnp.zeros(plan.tile, f32) for _ in range(2)] for _ in range(2)]
        for n in range(plan.group):
            for sign, i, side, j, field, _ in plan.tiles():
                slot = n * plan.half + sign * plan.quad + i
                shift = 2 * slot - (lanes - 2 if side == 0 else 0)
                value = rotate((f_ref, g_ref)[field][at * plan.group + n, j], shift, 1)
                packed[side][field] = jnp.where(pair_lane == slot, value, packed[side][field])
        for side in range(2):
            for field in range(2):
                where = field * plan.groups + at
                value = packed[side][field]
                col_ref[side, where] = value
                top, bottom = value[rows - 1 : rows], value[0:1]
                even_ref[side, pl.ds(where, 1), :] = jnp.where(upward, top, bottom)
                odd_ref[side, pl.ds(where, 1), :] = jnp.where(upward, bottom, top)
        return 0

    lax.fori_loop(0, plan.groups, part, 0)


def forward_kernel(plan, even_ref, odd_ref, col_ref, corner_even, corner_odd, rows_ref, corner_ref, fwd_even, fwd_odd):
    parity, band = row_parity(), band_parity()
    rows_ref[1 - parity] = even_ref[...]
    rows_ref[parity] = odd_ref[...]
    corner_ref[1 - parity] = corner_even[...]
    corner_ref[parity] = corner_odd[...]
    for n, out in enumerate((fwd_even, fwd_odd)):
        top = band if n == 1 else 1 - band
        part = top * (plan.groups - 1)
        start = top * (plan.bins - FH) * plan.quad
        for sign in range(2):
            out[sign * plan.sent_rows : (sign + 1) * plan.sent_rows] = rows_ref[sign, pl.ds(start, plan.sent_rows)]
            for side in range(2):
                for field in range(2):
                    row = 4 * sign + 2 * side + field
                    at = field * plan.groups + part
                    out[plan.sent - 1, row : row + 1, :] = corner_ref[sign, side, pl.ds(at, 1), :]
                    out[2 * plan.sent_rows + 2 * side + field] = col_ref[side, at]


def side_columns(plan, speeds, sides, lane_table, here_at, corner_at, out_at):
    sub, lane = iotas(plan)
    rows, _ = plan.tile
    in_group = lane // plan.nd
    odd = lane % 2 == 1
    northward = (lane % plan.nd) // 2 < plan.quad
    speed = jnp.where(in_group == 0, speeds[0], jnp.where(in_group == 1, speeds[1], speeds[2]))
    ua, va = (speed * weight for weight in lane_table)
    stay = 1.0 - ua - va
    for side in range(2):
        near, corner_masks = sides[side]
        for field in range(2):
            here = here_at(side, field)
            below, above = (spread(corner_at(sign, side, field), plan) for sign in range(2))
            across = rotate(here, 1 if side == 0 else -1, 1)
            along = jnp.where(
                northward,
                jnp.where(sub == 0, below, rotate(here, 1, 0)),
                jnp.where(sub == rows - 1, above, rotate(here, -1, 0)),
            )
            after = near * (stay * here + ua * across + va * along)
            corner = jnp.where(northward, corner_masks[0] * below, corner_masks[1] * above)
            after = after + va * corner
            if side == 0:
                out_at(side, field, jnp.where(odd, here, rotate(after, -1, 1)))
            else:
                out_at(side, field, jnp.where(odd, rotate(after, 1, 1), here))


def side_masks(plan, row_masks, col_ref):
    sub, _ = iotas(plan)
    rows, lanes = plan.tile
    sides = []
    for side in range(2):
        edge = lanes - 1 if side == 0 else 0
        own = lanes - 1 - edge
        near = spread(col_ref[side, 2 * plan.groups, :, edge : edge + 1], plan)
        corners = [
            jnp.where(sub == (0, rows - 1)[sign], spread(row_masks[sign][0:1, own : own + 1], plan), 0.0)
            for sign in range(2)
        ]
        sides.append((near, corners))
    return sides


def sweep(plan, count, mask, row_masks, weight_at, field_at, halo_at, column_at, store, scratch):
    rows_after, *rest = scratch
    columns_ref, first_ref, after_ref, second_ref = (rest[n * STAGES : (n + 1) * STAGES] for n in range(4))
    sub, lane = iotas(plan)
    rows, lanes = plan.tile
    first_half = sub < rows // 2
    outer = (first_half & (lane == 0)) | (~first_half & (lane == lanes - 1))
    edge_row, step_row = (0, rows - 1), (1, -1)
    near_lane, into = (0, lanes - 1), (1, -1)

    def weights(k, i):
        return [spread(weight_at(k, *divmod(3 * i + c, rows)), plan) for c in range(3)]

    def beside(x, halo, sign, side, field):
        inner = 4 * side + 2 * field + 1 - sign
        return jnp.where(sub == edge_row[sign], spread(halo(inner), plan), rotate(x, step_row[sign], 0))

    def gather(k, slot):
        columns = [[column_at(k, side, field) for field in range(2)] for side in range(2)]
        for sign, i, side, j, field, at in plan.tiles():
            lane_at = 2 * (sign * plan.quad + i)
            shift = -(lane_at + 1) if side == 0 else lanes - 1 - lane_at
            column = rotate(columns[side][field], shift, 1)
            columns_ref[slot][at] = column
            moved = rotate(field_at(field, k, j), into[side], 1)
            first_ref[slot][at] = jnp.where(lane == near_lane[side], column, moved)
        for i in range(plan.quad):
            stay, u, v = weights(k, i)
            for sign in range(2):
                halo = halo_at(sign, k, i)[...]
                across = jnp.where(first_half, rotate(halo, 1, 1), rotate(halo, -1, 1))
                across = jnp.where(outer, 0.0, across)
                along = rotate(halo, step_row[sign], 0)
                rows_after[sign, k * plan.quad + i] = row_masks[sign] * (stay * halo + u * across + v * along)

    def first(k, slot):
        for sign, i, side, j, field, at in plan.tiles():
            stay, u, v = weights(k, i)
            x = field_at(field, k, j)
            halo = halo_at(sign, k, i)
            y = beside(x, lambda n: halo[n : n + 1, :], sign, side, field)
            x = mask * (stay * x + u * first_ref[slot][at] + v * y)
            after_ref[slot][at] = x
            far = lanes - 1 - near_lane[side]
            second_ref[slot][at] = rotate(jnp.where(lane == far, columns_ref[slot][at], x), into[side], 1)

    def second(k, slot):
        for sign, i, side, j, field, at in plan.tiles():
            stay, u, v = weights(k, i)
            x = after_ref[slot][at]
            halo = rows_after.at[sign, k * plan.quad + i]
            y = beside(x, lambda n: halo[n : n + 1, :], sign, side, field)
            store(field, k, j, mask * (stay * x + u * second_ref[slot][at] + v * y))

    def clamp(k):
        return jnp.clip(k, 0, count - 1)

    def turn(t, _):
        for n in range(STAGES):
            at = t * STAGES + n
            second(clamp(at - 2), (n - 2) % STAGES)
            first(clamp(at - 1), (n - 1) % STAGES)
            gather(clamp(at), n)
        return 0

    lax.fori_loop(0, -(-(count + 2) // STAGES), turn, 0)


def sweep_scratch(plan, count):
    return [pltpu.VMEM((2, count * plan.quad) + plan.tile, f32)] + [
        pltpu.VMEM((2 * plan.nd,) + plan.tile, f32)
    ] * (4 * STAGES)


def halo_masks(plan, rows_ref):
    rows = plan.rows
    return [spread(rows_ref[0, plan.last, rows - 1 : rows, :], plan), spread(rows_ref[1, plan.last, 0:1, :], plan)]


def turned(plan, tile, place):
    back = lax.rem(plan.lanes - place * plan.nd, plan.lanes)
    return pltpu.roll(tile, back, 1)


def own_kernel(plan, bands, f_ref, g_ref, mask_ref, rows_ref, col_ref, corner_ref, weight_ref, ext_ref, both_ref, *scratch):
    row_masks = halo_masks(plan, rows_ref)
    sides = side_masks(plan, row_masks, col_ref)
    lane_table = lane_weights(plan)
    for part in range(plan.groups):

        def put(side, field, value):
            both_ref[side, field, part] = value

        side_columns(
            plan, [level_speed(plan, bands, part * plan.group + n) for n in range(plan.group)], sides, lane_table,
            lambda side, field: col_ref[side, field * plan.groups + part],
            lambda sign, side, field: corner_ref[sign, side, pl.ds(field * plan.groups + part, 1), :],
            put,
        )

    def store(field, k, j, value):
        ext_ref[field, (FH + k) * plan.nd + j] = value

    sweep(
        plan, plan.bins, mask_ref[...].astype(f32), row_masks,
        lambda k, t, row: weight_ref[FH + k, t, row : row + 1, :],
        lambda field, k, j: (f_ref, g_ref)[field][k, j],
        lambda sign, k, i: rows_ref.at[sign, k * plan.quad + i],
        lambda k, side, field: turned(plan, both_ref[side, field, lax.div(k, plan.group)], lax.rem(k, plan.group)),
        store, scratch,
    )


def halo_kernel(
    plan, bands, raw_even, raw_odd, fwd_even, fwd_odd, mask_ref, rows_ref, col_ref, weight_ref, ext_in,
    ext_ref, raw_ref, fwd_ref, both_ref, *scratch,
):
    band = band_parity()
    for field in range(2):
        raw_ref[field, pl.ds((1 - band) * FH, FH)] = raw_even[field]
        raw_ref[field, pl.ds(band * FH, FH)] = raw_odd[field]
    fwd_ref[1 - band] = fwd_even[...]
    fwd_ref[band] = fwd_odd[...]
    row_masks = halo_masks(plan, rows_ref)
    sides = side_masks(plan, row_masks, col_ref)
    lane_table = lane_weights(plan)
    for part in range(2):

        def put(side, field, value):
            both_ref[side, field, part] = value

        def corner(sign, side, field):
            row = 4 * sign + 2 * side + field
            return fwd_ref[part, plan.sent - 1, row : row + 1, :]

        side_columns(
            plan, [level_speed(plan, bands, part * (FH + plan.bins) - FH + n) for n in range(plan.group)], sides, lane_table,
            lambda side, field: fwd_ref[part, 2 * plan.sent_rows + 2 * side + field],
            corner,
            put,
        )

    def level(k):
        return jnp.where(k < FH, k, k + plan.bins)

    def store(field, k, j, value):
        ext_ref[field, level(k) * plan.nd + j] = value

    def halo(sign, k, i):
        part = jnp.where(k < FH, 0, 1)
        return fwd_ref.at[part, sign * plan.sent_rows + (k - part * FH) * plan.quad + i]

    def column(k, side, field):
        part = jnp.where(k < FH, 0, 1)
        return turned(plan, both_ref[side, field, part], k - part * FH)

    sweep(
        plan, 2 * FH, mask_ref[...].astype(f32), row_masks,
        lambda k, t, row: weight_ref[level(k), t, row : row + 1, :],
        lambda field, k, j: raw_ref[field, k, j],
        halo, column, store, scratch,
    )


def source_levels(plan, freq_ref, dir_ref, coupling_ref, ext_ref, fo_ref, go_ref, first, last):
    bins, nd = plan.bins, plan.nd
    p, q = freq_ref[0], freq_ref[1]
    e, h = dir_ref[0], dir_ref[1]
    span = (bins - 1) * nd + 1

    def wrap(j):
        return jnp.where(j >= nd, j - nd, jnp.where(j < 0, j + nd, j))

    def direction(j, _):
        def at(field, level, where):
            return ext_ref.at[field, pl.ds(level * nd + where, span)]

        own = [at(field, FH, j) for field in range(2)]
        up_one = [at(field, FH + p, wrap(j + e)) for field in range(2)]
        up_two = [at(field, FH + p, wrap(j - e)) for field in range(2)]
        low_one = [at(field, FH - q, wrap(j - h)) for field in range(2)]
        low_two = [at(field, FH - q, wrap(j + h)) for field in range(2)]
        out_f, out_g = (ref.at[pl.ds(j, span)] for ref in (fo_ref, go_ref))
        for k in range(bins):
            n = k * nd
            strength = source_step * coupling_ref[k]
            f0, g0 = own[0][n], own[1][n]
            fp1, gp1 = up_one[0][n], up_one[1][n]
            fp2, gp2 = up_two[0][n], up_two[1][n]
            fm1, gm1 = low_one[0][n], low_one[1][n]
            fm2, gm2 = low_two[0][n], low_two[1][n]
            linear = weight_plus * (fp1 + fp2) + weight_minus * (fm1 + fm2)
            linear_t = weight_plus * (gp1 + gp2) + weight_minus * (gm1 + gm2)
            cross = weight_cross * (fp1 * fm1 + fp2 * fm2)
            cross_t = weight_cross * ((gp1 * fm1 + fp1 * gm1) + (gp2 * fm2 + fp2 * gm2))
            f0l = f0 * linear
            both = f0l - cross
            rate = f0 * both
            change = g0 * (f0l + both) + f0 * (f0 * linear_t - cross_t)
            out_f[n] = f0 - strength * rate
            out_g[n] = g0 - strength * change
        return 0

    lax.fori_loop(first, last, direction, 0)


def flat(plan, ref):
    return ref.reshape((plan.bins * plan.nd,) + plan.tile)


def source_kernel(plan, freq_ref, dir_ref, coupling_ref, ext_ref, mask_ref, f_ref, g_ref, even_ref, odd_ref, raw_even, raw_odd, rows_ref):
    source_levels(plan, freq_ref, dir_ref, coupling_ref, ext_ref, flat(plan, f_ref), flat(plan, g_ref), 0, plan.nd)
    for sign in range(2):
        rows_ref[sign, plan.last] = mask_ref[...].astype(f32)
    lax.fori_loop(0, plan.bins, lambda k, _: pack_rows(plan, k, f_ref, g_ref, rows_ref) or 0, 0)
    send_out(plan, f_ref, g_ref, rows_ref, (even_ref, odd_ref), (raw_even, raw_odd))


def last_kernel(plan, chunks, freq_ref, dir_ref, coupling_ref, ext_ref, f_hbm, g_hbm, f_ref, g_ref, sems):
    each = plan.nd // chunks
    copies = []
    for n in range(chunks):
        source_levels(
            plan, freq_ref, dir_ref, coupling_ref, ext_ref, flat(plan, f_ref), flat(plan, g_ref), n * each, (n + 1) * each
        )
        part = pl.ds(n * each, each)
        for field, (src, dst) in enumerate(((f_ref, f_hbm), (g_ref, g_hbm))):
            copies.append(pltpu.make_async_copy(src.at[:, part], dst.at[:, part], sems.at[field, n]))
            copies[-1].start()
    for copy in copies:
        copy.wait()


def body(background, tangent, sea_mask, coupling, freq_offsets, dir_offsets):
    bins, nd = background.shape[:2]
    rows, lanes = background.shape[-2:]
    plan = Plan(bins, nd, rows, lanes)
    f = pltpu.with_memory_space_constraint(background.reshape(bins, nd, rows, lanes), pltpu.HBM)
    g = pltpu.with_memory_space_constraint(tangent.reshape(bins, nd, rows, lanes), pltpu.HBM)
    mask = sea_mask.reshape(rows, lanes)
    bands, tiles = lax.axis_size("band"), lax.axis_size("tile")

    def array(*shape):
        return jax.ShapeDtypeStruct(shape + plan.tile, f32)

    field = array(bins, nd)
    ext_out = array(2, plan.levels * nd)
    row_out = array(plan.last + 1)
    col_out = array(2, 2 * plan.groups + 1)
    corner_out = jax.ShapeDtypeStruct((2, -(-2 * plan.groups // 8) * 8, lanes), f32)
    raw_out = array(2, FH, nd)
    fwd_out = array(plan.sent)
    both = pltpu.VMEM((2, 2, plan.groups) + plan.tile, f32)
    sorted_rows = pltpu.VMEM((2, plan.last + 1) + plan.tile, f32)

    def kernel(function, out_shape, in_specs, scratch=(), out_specs=None, aliases={}, static=()):
        return pl.pallas_call(
            functools.partial(function, plan, *static),
            out_shape=out_shape,
            in_specs=in_specs,
            out_specs=out_specs or (VM,) * len(out_shape),
            scratch_shapes=list(scratch),
            input_output_aliases=aliases,
            compiler_params=pltpu.CompilerParams(vmem_limit_bytes=20 * 1024 * 1024),
        )

    def tile_pairs(parity, east):
        pairs = []
        for i in range(tiles):
            at = (i + TY // 2) % tiles
            row = at % TY
            if parity is not None:
                row += 1 if row % 2 == parity else -1
            if 0 <= row < TY:
                to = (at // TY * TY + row + east * TY) % tiles
                pairs.append((i, (to - TY // 2) % tiles))
        return pairs

    def tile_swap(value, parity):
        return lax.ppermute(value, "tile", tile_pairs(parity, 0))

    def sideways(value, parity):
        if tiles == 2 * TY:
            return lax.ppermute(value, "tile", tile_pairs(parity, 1))
        return jnp.concatenate(
            [lax.ppermute(value[n : n + 1], "tile", tile_pairs(parity, 1 - 2 * n)) for n in range(2)]
        )

    def band_swap(value, parity):
        pairs = [(i, i + 1 if i % 2 == parity else i - 1) for i in range(bands)]
        return lax.ppermute(value, "band", [(a, b) for a, b in pairs if 0 <= b < bands])

    f, g, even, odd, raw_even, raw_odd, weights = kernel(
        load_kernel,
        (field, field, row_out, row_out, raw_out, raw_out, array(plan.levels, plan.weight_tiles)),
        [HBM, HBM, VM],
        [sorted_rows, pltpu.SemaphoreType.DMA((2, bins))],
        static=(bands,),
    )(f, g, mask)

    for step in range(STEPS):
        odd = tile_swap(odd, 1)
        even = tile_swap(even, 0)
        raw_odd = band_swap(raw_odd, 1)
        raw_even = band_swap(raw_even, 0)
        cols, corner_even, corner_odd = kernel(pack_kernel, (col_out, corner_out, corner_out), [VM] * 3)(f, g, mask)
        cols = sideways(cols, None)
        corner_odd = sideways(corner_odd, 1)
        corner_even = sideways(corner_even, 0)
        sorted_out = (array(2, plan.last + 1), jax.ShapeDtypeStruct((2,) + corner_out.shape, f32), fwd_out, fwd_out)
        halo_rows, corners, fwd_even, fwd_odd = kernel(forward_kernel, sorted_out, [VM] * 5)(
            even, odd, cols, corner_even, corner_odd
        )
        fwd_odd = band_swap(fwd_odd, 1)
        fwd_even = band_swap(fwd_even, 0)
        (ext,) = kernel(
            own_kernel, (ext_out,), [VM] * 7, [both] + sweep_scratch(plan, bins), static=(bands,)
        )(f, g, mask, halo_rows, cols, corners, weights)
        (ext,) = kernel(
            halo_kernel,
            (ext_out,),
            [VM] * 9,
            [pltpu.VMEM((2, 2 * FH, nd) + plan.tile, f32), pltpu.VMEM((2, plan.sent) + plan.tile, f32), both]
            + sweep_scratch(plan, 2 * FH),
            aliases={8: 0},
            static=(bands,),
        )(raw_even, raw_odd, fwd_even, fwd_odd, mask, halo_rows, cols, weights, ext)
        if step < STEPS - 1:
            f, g, even, odd, raw_even, raw_odd = kernel(
                source_kernel, (field, field, row_out, row_out, raw_out, raw_out), [SM] * 3 + [VM] * 2, [sorted_rows]
            )(freq_offsets, dir_offsets, coupling, ext, mask)
        else:
            chunks = 6
            f, g = kernel(
                lambda plan, *refs: last_kernel(plan, chunks, *refs),
                (field, field),
                [SM] * 3 + [VM],
                [pltpu.VMEM(field.shape, f32)] * 2 + [pltpu.SemaphoreType.DMA((2, chunks))],
                out_specs=(HBM, HBM),
            )(freq_offsets, dir_offsets, coupling, ext)
    return f.reshape(background.shape), g.reshape(tangent.shape)


def solution(mesh):
    in_specs = (
        P("band", None, "tile", None, None),
        P("band", None, "tile", None, None),
        P("tile", None, None),
        P("band"),
        P(),
        P(),
    )
    out_specs = (P("band", None, "tile", None, None), P("band", None, "tile", None, None))
    return jax.shard_map(body, mesh=mesh, in_specs=in_specs, out_specs=out_specs, check_vma=False)
```

profile of v0, /device:TPU:1, one launch (start us, length us, event | category | flops | bytes accessed | tf_op | source)
XLA Modules:
  0.0 94.1 jit_solution(16043045568744341272)
XLA Ops:
  0.6 0.7 copy-done
  1.3 2.3 %shard_map.77 = (f32[9,36,8,128]{3,2,1,0:T(8,128)S(1)}, f32[9,36,8,128]{3,2,1,0:T(8,128)S(1)}, f32[82,8,128]{2,1,0:T(8,128)S(1)}, f32[82,8,128]{2,1,0:T(8,128)S(...) custom-call(f32[9,36,8,128]{3,2,1,0:T(8,128)} %bitcast.17, ...), custom_call_target="tpu_custom_call" | custom-call | tf_op jit(solution)/shard_map/pallas_call | solution.py:546
  3.7 4.5 %collective-permute-start.1 = (f32[2,3,36,8,128]{4,3,2,1,0:T(8,128)S(1)}, f32[2,3,36,8,128]{4,3,2,1,0:T(8,128)S(1)}, u32[]{:S(2)}, u32[]{:S(2)}) collective-permute-start(f32[2,3,36,8,128]{4,3,2,1,0:T(8,128)S(1)} %get-tuple-element.32), channel_id=1, source_target_pairs={{1,2},{2,1},{5,6},{6,5},{9,10},{10,9},{13,14},{14,13},{17,18},{18,... | collective-permute-start | bytes 2654216 | tf_op jit(solution)/shard_map/ppermute | solution.py:544
  8.2 1.3 %collective-permute-start.2 = (f32[82,8,128]{2,1,0:T(8,128)S(1)}, f32[82,8,128]{2,1,0:T(8,128)S(1)}, u32[]{:S(2)}, u32[]{:S(2)}) collective-permute-start(f32[82,8,128]{2,1,0:T(8,128)S(1)} %get-tuple-element.33), channel_id=1, source_target_pairs={{0,4},{4,0},{8,12},{12,8},{16,20},{20,16},{24,28},{28,24},{1,5},{5... | collective-permute-start | bytes 1007624 | tf_op jit(solution)/shard_map/ppermute | solution.py:533
  9.5 5.2 %collective-permute-start.3 = (f32[82,8,128]{2,1,0:T(8,128)S(1)}, f32[82,8,128]{2,1,0:T(8,128)S(1)}, u32[]{:S(2)}, u32[]{:S(2)}) collective-permute-start(f32[82,8,128]{2,1,0:T(8,128)S(1)} %get-tuple-element.34), channel_id=1, source_target_pairs={{0,28},{12,16},{16,12},{28,0},{1,29},{13,17},{17,13},{29,1},{2,30}... | collective-permute-start | bytes 1007624 | tf_op jit(solution)/shard_map/ppermute | solution.py:533
  14.7 0.9 shard_map.78
  15.7 6.8 %collective-permute-done.5.corner_even = f32[2,8,128]{2,1,0:T(8,128)S(1)} collective-permute-done((f32[2,8,128]{2,1,0:T(8,128)S(1)}, f32[2,8,128]{2,1,0:T(8,128)S(1)}, u32[]{:S(2)}, u32[]{:S(2)}) %collective-permute-start.5) | collective-permute-done | bytes 8224 | tf_op jit(solution)/shard_map/ppermute | solution.py:537
  22.5 1.9 %collective-permute-start.6 = (f32[2,8,128]{2,1,0:T(8,128)S(1)}, f32[2,8,128]{2,1,0:T(8,128)S(1)}, u32[]{:S(2)}, u32[]{:S(2)}) collective-permute-start(f32[2,8,128]{2,1,0:T(8,128)S(1)} %get-tuple-element.39), channel_id=1, source_target_pairs={{0,12},{12,0},{16,28},{28,16},{1,13},{13,1},{17,29},{29,17},{2,14}... | collective-permute-start | bytes 24584 | tf_op jit(solution)/shard_map/ppermute | solution.py:537
  24.4 3.4 %collective-permute-done.6.corner_odd = f32[2,8,128]{2,1,0:T(8,128)S(1)} collective-permute-done((f32[2,8,128]{2,1,0:T(8,128)S(1)}, f32[2,8,128]{2,1,0:T(8,128)S(1)}, u32[]{:S(2)}, u32[]{:S(2)}) %collective-permute-start.6) | collective-permute-done | bytes 8224 | tf_op jit(solution)/shard_map/ppermute | solution.py:537
  27.8 1.2 %collective-permute-start.4 = (f32[2,7,8,128]{3,2,1,0:T(8,128)S(1)}, f32[2,7,8,128]{3,2,1,0:T(8,128)S(1)}, u32[]{:S(2)}, u32[]{:S(2)}) collective-permute-start(f32[2,7,8,128]{3,2,1,0:T(8,128)S(1)} %get-tuple-element.37), channel_id=1, source_target_pairs={{0,16},{4,20},{8,24},{12,28},{16,0},{20,4},{24,8},{28,12},{1,17},{... | collective-permute-start | bytes 172040 | tf_op jit(solution)/shard_map/ppermute | solution.py:537
  29.0 3.6 %collective-permute-done.4.col_ref = f32[2,7,8,128]{3,2,1,0:T(8,128)S(1)} collective-permute-done((f32[2,7,8,128]{3,2,1,0:T(8,128)S(1)}, f32[2,7,8,128]{3,2,1,0:T(8,128)S(1)}, u32[]{:S(2)}, u32[]{:S(2)}) %collective-permute-start.4) | collective-permute-done | bytes 57376 | tf_op jit(solution)/shard_map/ppermute | solution.py:537
  32.6 0.1 shard_map.79
  32.7 0.5 collective-permute-start.7
  33.2 3.9 %collective-permute-start.8 = (f32[59,8,128]{2,1,0:T(8,128)S(1)}, f32[59,8,128]{2,1,0:T(8,128)S(1)}, u32[]{:S(2)}, u32[]{:S(2)}) collective-permute-start(f32[59,8,128]{2,1,0:T(8,128)S(1)} %get-tuple-element.41), channel_id=1, source_target_pairs={{1,2},{2,1},{5,6},{6,5},{9,10},{10,9},{13,14},{14,13},{17,18},{18,... | collective-permute-start | bytes 725000 | tf_op jit(solution)/shard_map/ppermute | solution.py:544
  37.2 5.6 %shard_map.80.ext_in = f32[2,540,8,128]{3,2,1,0:T(8,128)S(1)} custom-call(f32[9,36,8,128]{3,2,1,0:T(8,128)S(1)} %get-tuple-element.35.f_ref, f32[9,36,8,128]{3,2,1,0:T(8,128)S(1)} %get-tuple-element.36.g_ref, s32[8,128]{1,0:T(8,128)S(1)} %bitcast.11, f32[2,82,8,128]{3,2,1,0:T(8,128)S(1)} %get-tuple-element.42.rows_ref, ...), custom_call_target="tpu_custom_call" | custom-call | tf_op jit(solution)/shard_map/pallas_call | solution.py:569
  42.8 3.8 %shard_map.81.ext_ref = f32[2,540,8,128]{3,2,1,0:T(8,128)S(1)} custom-call(f32[2,3,36,8,128]{4,3,2,1,0:T(8,128)S(1)} %collective-permute-done.raw_even, f32[2,3,36,8,128]{4,3,2,1,0:T(8,128)S(1)} %collective-permute-done.1.raw_odd, f32[59,8,128]{2,1,0:T(8,128)S(1)} %collective-permute-done.7.fwd_even, ...), custom_call_target="tpu_custom_call", output_to_operand_aliasing={{}: (8, {})} | custom-call | tf_op jit(solution)/shard_map/pallas_call | solution.py:572
  46.7 3.4 %shard_map.82 = (f32[9,36,8,128]{3,2,1,0:T(8,128)S(1)}, f32[9,36,8,128]{3,2,1,0:T(8,128)S(1)}, f32[82,8,128]{2,1,0:T(8,128)S(1)}, f32[82,8,128]{2,1,0:T(8,128)S(...) custom-call(s32[2]{0:T(128)S(1)} %copy-done.2, s32[2]{0:T(128)S(1)} %copy-done.3, ...), custom_call_target="tpu_custom_call" | custom-call | tf_op jit(solution)/shard_map/pallas_call | solution.py:582
  50.2 1.9 %collective-permute-start.10 = (f32[2,3,36,8,128]{4,3,2,1,0:T(8,128)S(1)}, f32[2,3,36,8,128]{4,3,2,1,0:T(8,128)S(1)}, u32[]{:S(2)}, u32[]{:S(2)}) collective-permute-start(f32[2,3,36,8,128]{4,3,2,1,0:T(8,128)S(1)} %get-tuple-element.46), channel_id=1, source_target_pairs={{1,2},{2,1},{5,6},{6,5},{9,10},{10,9},{13,14},{14,13},{17,18},{18,... | collective-permute-start | bytes 2654216 | tf_op jit(solution)/shard_map/ppermute | solution.py:544
  52.2 5.2 %collective-permute-start.12 = (f32[82,8,128]{2,1,0:T(8,128)S(1)}, f32[82,8,128]{2,1,0:T(8,128)S(1)}, u32[]{:S(2)}, u32[]{:S(2)}) collective-permute-start(f32[82,8,128]{2,1,0:T(8,128)S(1)} %get-tuple-element.48), channel_id=1, source_target_pairs={{0,28},{12,16},{16,12},{28,0},{1,29},{13,17},{17,13},{29,1},{2,30}... | collective-permute-start | bytes 1007624 | tf_op jit(solution)/shard_map/ppermute | solution.py:533
  57.4 0.9 shard_map.83
  58.4 8.4 %collective-permute-done.14.corner_even = f32[2,8,128]{2,1,0:T(8,128)S(1)} collective-permute-done((f32[2,8,128]{2,1,0:T(8,128)S(1)}, f32[2,8,128]{2,1,0:T(8,128)S(1)}, u32[]{:S(2)}, u32[]{:S(2)}) %collective-permute-start.14) | collective-permute-done | bytes 8224 | tf_op jit(solution)/shard_map/ppermute | solution.py:537
  66.8 1.9 %collective-permute-start.15 = (f32[2,8,128]{2,1,0:T(8,128)S(1)}, f32[2,8,128]{2,1,0:T(8,128)S(1)}, u32[]{:S(2)}, u32[]{:S(2)}) collective-permute-start(f32[2,8,128]{2,1,0:T(8,128)S(1)} %get-tuple-element.53), channel_id=1, source_target_pairs={{0,12},{12,0},{16,28},{28,16},{1,13},{13,1},{17,29},{29,17},{2,14}... | collective-permute-start | bytes 24584 | tf_op jit(solution)/shard_map/ppermute | solution.py:537
  68.7 3.4 %collective-permute-done.15.corner_odd = f32[2,8,128]{2,1,0:T(8,128)S(1)} collective-permute-done((f32[2,8,128]{2,1,0:T(8,128)S(1)}, f32[2,8,128]{2,1,0:T(8,128)S(1)}, u32[]{:S(2)}, u32[]{:S(2)}) %collective-permute-start.15) | collective-permute-done | bytes 8224 | tf_op jit(solution)/shard_map/ppermute | solution.py:537
  72.1 1.2 %collective-permute-start.13 = (f32[2,7,8,128]{3,2,1,0:T(8,128)S(1)}, f32[2,7,8,128]{3,2,1,0:T(8,128)S(1)}, u32[]{:S(2)}, u32[]{:S(2)}) collective-permute-start(f32[2,7,8,128]{3,2,1,0:T(8,128)S(1)} %get-tuple-element.51), channel_id=1, source_target_pairs={{0,16},{4,20},{8,24},{12,28},{16,0},{20,4},{24,8},{28,12},{1,17},{... | collective-permute-start | bytes 172040 | tf_op jit(solution)/shard_map/ppermute | solution.py:537
  73.3 2.7 %collective-permute-done.13.col_ref = f32[2,7,8,128]{3,2,1,0:T(8,128)S(1)} collective-permute-done((f32[2,7,8,128]{3,2,1,0:T(8,128)S(1)}, f32[2,7,8,128]{3,2,1,0:T(8,128)S(1)}, u32[]{:S(2)}, u32[]{:S(2)}) %collective-permute-start.13) | collective-permute-done | bytes 57376 | tf_op jit(solution)/shard_map/ppermute | solution.py:537
  76.0 0.1 shard_map.84
  76.2 2.8 %collective-permute-start.16 = (f32[59,8,128]{2,1,0:T(8,128)S(1)}, f32[59,8,128]{2,1,0:T(8,128)S(1)}, u32[]{:S(2)}, u32[]{:S(2)}) collective-permute-start(f32[59,8,128]{2,1,0:T(8,128)S(1)} %get-tuple-element.54), channel_id=1, source_target_pairs={{0,1},{1,0},{2,3},{3,2},{4,5},{5,4},{6,7},{7,6},{8,9},{9,8},{10,11... | collective-permute-start | bytes 725000 | tf_op jit(solution)/shard_map/ppermute | solution.py:544
  78.9 1.9 %collective-permute-start.17 = (f32[59,8,128]{2,1,0:T(8,128)S(1)}, f32[59,8,128]{2,1,0:T(8,128)S(1)}, u32[]{:S(2)}, u32[]{:S(2)}) collective-permute-start(f32[59,8,128]{2,1,0:T(8,128)S(1)} %get-tuple-element.55), channel_id=1, source_target_pairs={{1,2},{2,1},{5,6},{6,5},{9,10},{10,9},{13,14},{14,13},{17,18},{18,... | collective-permute-start | bytes 725000 | tf_op jit(solution)/shard_map/ppermute | solution.py:544
  80.8 5.4 %shard_map.85.ext_in = f32[2,540,8,128]{3,2,1,0:T(8,128)S(1)} custom-call(f32[9,36,8,128]{3,2,1,0:T(8,128)S(1)} %get-tuple-element.49.f_ref, f32[9,36,8,128]{3,2,1,0:T(8,128)S(1)} %get-tuple-element.50.g_ref, s32[8,128]{1,0:T(8,128)S(1)} %bitcast.15, f32[2,82,8,128]{3,2,1,0:T(8,128)S(1)} %get-tuple-element.56.rows_ref, ...), custom_call_target="tpu_custom_call" | custom-call | tf_op jit(solution)/shard_map/pallas_call | solution.py:569
  86.3 0.1 collective-permute-done.17.fwd_odd
  86.4 3.8 %shard_map.86.refs_3_ = f32[2,540,8,128]{3,2,1,0:T(8,128)S(1)} custom-call(f32[2,3,36,8,128]{4,3,2,1,0:T(8,128)S(1)} %collective-permute-done.9.raw_even, f32[2,3,36,8,128]{4,3,2,1,0:T(8,128)S(1)} %collective-permute-done.10.raw_odd, f32[59,8,128]{2,1,0:T(8,128)S(1)} %collective-permute-done.16.fwd_even, ...), custom_call_target="tpu_custom_call", output_to_operand_aliasing={{}: (8, {})} | custom-call | tf_op jit(solution)/shard_map/pallas_call | solution.py:572
  90.2 3.9 %shard_map.87 = (f32[9,36,8,128]{3,2,1,0:T(8,128)}, f32[9,36,8,128]{3,2,1,0:T(8,128)}) custom-call(s32[2]{0:T(128)S(1)} %copy-done.2, s32[2]{0:T(128)S(1)} %copy-done.3, f32[9]{0:T(128)S(1)} %copy-done.4, f32[2,540,8,128]{3,2,1,0:T(8,128)S(1)} %shard_map.86.refs_3_), custom_call_target="tpu_custom_call" | custom-call | tf_op jit(solution)/shard_map/pallas_call | solution.py:587
  (25 shorter events, 0.4 us)
Async XLA Ops:
  0.6 0.7 copy-start
  3.6 39.2 %collective-permute-start = (f32[2,3,36,8,128]{4,3,2,1,0:T(8,128)S(1)}, f32[2,3,36,8,128]{4,3,2,1,0:T(8,128)S(1)}, u32[]{:S(2)}, u32[]{:S(2)}) collective-permute-start(f32[2,3,36,8,128]{4,3,2,1,0:T(8,128)S(1)} %get-tuple-element.31), channel_id=1, source_target_pairs={{0,1},{1,0},{2,3},{3,2},{4,5},{5,4},{6,7},{7,6},{8,9},{9,8},{10,11... | collective-permute-start | bytes 2654216 | tf_op jit(solution)/shard_map/ppermute | solution.py:544
  3.7 39.1 %collective-permute-start.1 = (f32[2,3,36,8,128]{4,3,2,1,0:T(8,128)S(1)}, f32[2,3,36,8,128]{4,3,2,1,0:T(8,128)S(1)}, u32[]{:S(2)}, u32[]{:S(2)}) collective-permute-start(f32[2,3,36,8,128]{4,3,2,1,0:T(8,128)S(1)} %get-tuple-element.32), channel_id=1, source_target_pairs={{1,2},{2,1},{5,6},{6,5},{9,10},{10,9},{13,14},{14,13},{17,18},{18,... | collective-permute-start | bytes 2654216 | tf_op jit(solution)/shard_map/ppermute | solution.py:544
  8.2 24.4 %collective-permute-start.2 = (f32[82,8,128]{2,1,0:T(8,128)S(1)}, f32[82,8,128]{2,1,0:T(8,128)S(1)}, u32[]{:S(2)}, u32[]{:S(2)}) collective-permute-start(f32[82,8,128]{2,1,0:T(8,128)S(1)} %get-tuple-element.33), channel_id=1, source_target_pairs={{0,4},{4,0},{8,12},{12,8},{16,20},{20,16},{24,28},{28,24},{1,5},{5... | collective-permute-start | bytes 1007624 | tf_op jit(solution)/shard_map/ppermute | solution.py:533
  9.5 23.1 %collective-permute-start.3 = (f32[82,8,128]{2,1,0:T(8,128)S(1)}, f32[82,8,128]{2,1,0:T(8,128)S(1)}, u32[]{:S(2)}, u32[]{:S(2)}) collective-permute-start(f32[82,8,128]{2,1,0:T(8,128)S(1)} %get-tuple-element.34), channel_id=1, source_target_pairs={{0,28},{12,16},{16,12},{28,0},{1,29},{13,17},{17,13},{29,1},{2,30}... | collective-permute-start | bytes 1007624 | tf_op jit(solution)/shard_map/ppermute | solution.py:533
  15.6 6.9 %collective-permute-start.5 = (f32[2,8,128]{2,1,0:T(8,128)S(1)}, f32[2,8,128]{2,1,0:T(8,128)S(1)}, u32[]{:S(2)}, u32[]{:S(2)}) collective-permute-start(f32[2,8,128]{2,1,0:T(8,128)S(1)} %get-tuple-element.38), channel_id=1, source_target_pairs={{0,20},{4,16},{8,28},{12,24},{16,4},{20,0},{24,12},{28,8},{1,21},{... | collective-permute-start | bytes 24584 | tf_op jit(solution)/shard_map/ppermute | solution.py:537
  22.5 5.3 %collective-permute-start.6 = (f32[2,8,128]{2,1,0:T(8,128)S(1)}, f32[2,8,128]{2,1,0:T(8,128)S(1)}, u32[]{:S(2)}, u32[]{:S(2)}) collective-permute-start(f32[2,8,128]{2,1,0:T(8,128)S(1)} %get-tuple-element.39), channel_id=1, source_target_pairs={{0,12},{12,0},{16,28},{28,16},{1,13},{13,1},{17,29},{29,17},{2,14}... | collective-permute-start | bytes 24584 | tf_op jit(solution)/shard_map/ppermute | solution.py:537
  27.8 4.8 %collective-permute-start.4 = (f32[2,7,8,128]{3,2,1,0:T(8,128)S(1)}, f32[2,7,8,128]{3,2,1,0:T(8,128)S(1)}, u32[]{:S(2)}, u32[]{:S(2)}) collective-permute-start(f32[2,7,8,128]{3,2,1,0:T(8,128)S(1)} %get-tuple-element.37), channel_id=1, source_target_pairs={{0,16},{4,20},{8,24},{12,28},{16,0},{20,4},{24,8},{28,12},{1,17},{... | collective-permute-start | bytes 172040 | tf_op jit(solution)/shard_map/ppermute | solution.py:537
  32.7 10.1 %collective-permute-start.7 = (f32[59,8,128]{2,1,0:T(8,128)S(1)}, f32[59,8,128]{2,1,0:T(8,128)S(1)}, u32[]{:S(2)}, u32[]{:S(2)}) collective-permute-start(f32[59,8,128]{2,1,0:T(8,128)S(1)} %get-tuple-element.40), channel_id=1, source_target_pairs={{0,1},{1,0},{2,3},{3,2},{4,5},{5,4},{6,7},{7,6},{8,9},{9,8},{10,11... | collective-permute-start | bytes 725000 | tf_op jit(solution)/shard_map/ppermute | solution.py:544
  33.2 9.6 %collective-permute-start.8 = (f32[59,8,128]{2,1,0:T(8,128)S(1)}, f32[59,8,128]{2,1,0:T(8,128)S(1)}, u32[]{:S(2)}, u32[]{:S(2)}) collective-permute-start(f32[59,8,128]{2,1,0:T(8,128)S(1)} %get-tuple-element.41), channel_id=1, source_target_pairs={{1,2},{2,1},{5,6},{6,5},{9,10},{10,9},{13,14},{14,13},{17,18},{18,... | collective-permute-start | bytes 725000 | tf_op jit(solution)/shard_map/ppermute | solution.py:544
  42.7 3.9 %copy-start.1 = (s32[1,8,128]{2,1,0:T(8,128)S(1)}, s32[1,8,128]{2,1,0:T(8,128)}, u32[]{:S(2)}) copy-start(s32[1,8,128]{2,1,0:T(8,128)} %param.8) | copy-start | bytes 12292
  42.8 3.9 %copy-start.2 = (s32[2]{0:T(128)S(1)}, s32[2]{0:T(128)}, u32[]{:S(2)}) copy-start(s32[2]{0:T(128)} %refs_0_.1) | copy-start | bytes 28
  42.8 3.9 %copy-start.3 = (s32[2]{0:T(128)S(1)}, s32[2]{0:T(128)}, u32[]{:S(2)}) copy-start(s32[2]{0:T(128)} %refs_1_.1) | copy-start | bytes 28
  42.8 3.9 %copy-start.4 = (f32[9]{0:T(128)S(1)}, f32[9]{0:T(128)}, u32[]{:S(2)}) copy-start(f32[9]{0:T(128)} %refs_2_.1) | copy-start | bytes 112
  50.2 36.2 %collective-permute-start.9 = (f32[2,3,36,8,128]{4,3,2,1,0:T(8,128)S(1)}, f32[2,3,36,8,128]{4,3,2,1,0:T(8,128)S(1)}, u32[]{:S(2)}, u32[]{:S(2)}) collective-permute-start(f32[2,3,36,8,128]{4,3,2,1,0:T(8,128)S(1)} %get-tuple-element.45), channel_id=1, source_target_pairs={{0,1},{1,0},{2,3},{3,2},{4,5},{5,4},{6,7},{7,6},{8,9},{9,8},{10,11... | collective-permute-start | bytes 2654216 | tf_op jit(solution)/shard_map/ppermute | solution.py:544
  50.2 36.1 %collective-permute-start.10 = (f32[2,3,36,8,128]{4,3,2,1,0:T(8,128)S(1)}, f32[2,3,36,8,128]{4,3,2,1,0:T(8,128)S(1)}, u32[]{:S(2)}, u32[]{:S(2)}) collective-permute-start(f32[2,3,36,8,128]{4,3,2,1,0:T(8,128)S(1)} %get-tuple-element.46), channel_id=1, source_target_pairs={{1,2},{2,1},{5,6},{6,5},{9,10},{10,9},{13,14},{14,13},{17,18},{18,... | collective-permute-start | bytes 2654216 | tf_op jit(solution)/shard_map/ppermute | solution.py:544
  52.2 23.9 %collective-permute-start.11 = (f32[82,8,128]{2,1,0:T(8,128)S(1)}, f32[82,8,128]{2,1,0:T(8,128)S(1)}, u32[]{:S(2)}, u32[]{:S(2)}) collective-permute-start(f32[82,8,128]{2,1,0:T(8,128)S(1)} %get-tuple-element.47), channel_id=1, source_target_pairs={{0,4},{4,0},{8,12},{12,8},{16,20},{20,16},{24,28},{28,24},{1,5},{5... | collective-permute-start | bytes 1007624 | tf_op jit(solution)/shard_map/ppermute | solution.py:533
  52.2 23.8 %collective-permute-start.12 = (f32[82,8,128]{2,1,0:T(8,128)S(1)}, f32[82,8,128]{2,1,0:T(8,128)S(1)}, u32[]{:S(2)}, u32[]{:S(2)}) collective-permute-start(f32[82,8,128]{2,1,0:T(8,128)S(1)} %get-tuple-element.48), channel_id=1, source_target_pairs={{0,28},{12,16},{16,12},{28,0},{1,29},{13,17},{17,13},{29,1},{2,30}... | collective-permute-start | bytes 1007624 | tf_op jit(solution)/shard_map/ppermute | solution.py:533
  58.3 8.5 %collective-permute-start.14 = (f32[2,8,128]{2,1,0:T(8,128)S(1)}, f32[2,8,128]{2,1,0:T(8,128)S(1)}, u32[]{:S(2)}, u32[]{:S(2)}) collective-permute-start(f32[2,8,128]{2,1,0:T(8,128)S(1)} %get-tuple-element.52), channel_id=1, source_target_pairs={{0,20},{4,16},{8,28},{12,24},{16,4},{20,0},{24,12},{28,8},{1,21},{... | collective-permute-start | bytes 24584 | tf_op jit(solution)/shard_map/ppermute | solution.py:537
  66.8 5.3 %collective-permute-start.15 = (f32[2,8,128]{2,1,0:T(8,128)S(1)}, f32[2,8,128]{2,1,0:T(8,128)S(1)}, u32[]{:S(2)}, u32[]{:S(2)}) collective-permute-start(f32[2,8,128]{2,1,0:T(8,128)S(1)} %get-tuple-element.53), channel_id=1, source_target_pairs={{0,12},{12,0},{16,28},{28,16},{1,13},{13,1},{17,29},{29,17},{2,14}... | collective-permute-start | bytes 24584 | tf_op jit(solution)/shard_map/ppermute | solution.py:537
  72.1 3.9 %collective-permute-start.13 = (f32[2,7,8,128]{3,2,1,0:T(8,128)S(1)}, f32[2,7,8,128]{3,2,1,0:T(8,128)S(1)}, u32[]{:S(2)}, u32[]{:S(2)}) collective-permute-start(f32[2,7,8,128]{3,2,1,0:T(8,128)S(1)} %get-tuple-element.51), channel_id=1, source_target_pairs={{0,16},{4,20},{8,24},{12,28},{16,0},{20,4},{24,8},{28,12},{1,17},{... | collective-permute-start | bytes 172040 | tf_op jit(solution)/shard_map/ppermute | solution.py:537
  76.2 10.1 %collective-permute-start.16 = (f32[59,8,128]{2,1,0:T(8,128)S(1)}, f32[59,8,128]{2,1,0:T(8,128)S(1)}, u32[]{:S(2)}, u32[]{:S(2)}) collective-permute-start(f32[59,8,128]{2,1,0:T(8,128)S(1)} %get-tuple-element.54), channel_id=1, source_target_pairs={{0,1},{1,0},{2,3},{3,2},{4,5},{5,4},{6,7},{7,6},{8,9},{9,8},{10,11... | collective-permute-start | bytes 725000 | tf_op jit(solution)/shard_map/ppermute | solution.py:544
  78.9 7.5 %collective-permute-start.17 = (f32[59,8,128]{2,1,0:T(8,128)S(1)}, f32[59,8,128]{2,1,0:T(8,128)S(1)}, u32[]{:S(2)}, u32[]{:S(2)}) collective-permute-start(f32[59,8,128]{2,1,0:T(8,128)S(1)} %get-tuple-element.55), channel_id=1, source_target_pairs={{1,2},{2,1},{5,6},{6,5},{9,10},{10,9},{13,14},{14,13},{17,18},{18,... | collective-permute-start | bytes 725000 | tf_op jit(solution)/shard_map/ppermute | solution.py:544
where the time goes:
time: 94.5 us; the launch traced here: 94.1 us
  starting transfers between devices  33.7 us (36%)
  Pallas kernels  30.3 us (32%)
  waiting for transfers between devices  28.4 us (30%)
    ppermute x6, waiting for transfers between devices, sideways(): return lax.ppermute(value, 'tile', tile_pairs(parity, 1))  28.3 us
    ppermute x8, starting transfers between devices, band_swap(): lax.ppermute(value, 'band', [(a, b) for a, b in pairs if 0 <= b < bands])  15.6 us
    ppermute x4, starting transfers between devices, tile_swap(): return lax.ppermute(value, 'tile', tile_pairs(parity, 0))  11.7 us
    pallas_call x2, Pallas kernels, body(): kernel(own_kernel, (ext_out,), [VM] * 7, [both] + sweep_scratch(plan, bin...  11 us
    pallas_call x2, Pallas kernels, body(): kernel(halo_kernel, (ext_out,), [VM] * 9, [pltpu.VMEM((2, 2 * FH, nd) + p...  7.69 us
    ppermute x6, starting transfers between devices, sideways(): return lax.ppermute(value, 'tile', tile_pairs(parity, 1))  6.37 us
    pallas_call x1, Pallas kernels, body(): kernel(lambda plan, *refs: last_kernel(plan, chunks, *refs), (field, fiel...  3.88 us
    pallas_call x1, Pallas kernels, body(): kernel(source_kernel, (field, field, row_out, row_out, raw_out, raw_out),...  3.42 us
  transfers between devices with their start and end apart: 18, of which 7 were waited for; matrix products, arithmetic and copies ran while one was open for 0% of the time, Pallas kernels for 14%

commit v1 on v0

--- a/solution.py
+++ b/solution.py
@@ -23,7 +23,6 @@
 SM = pl.BlockSpec(memory_space=pltpu.SMEM)
 HBM = pl.BlockSpec(memory_space=pltpu.HBM)
 f32 = jnp.float32
-STAGES = 2
 
 
 def rotate(x, shift, axis):
@@ -50,12 +49,11 @@
     def pair(self, sign, i):
         return (i, self.half - 1 - i) if sign == 0 else (self.nd - 1 - i, self.half + i)
 
-    def tiles(self):
-        for sign in range(2):
-            for i in range(self.quad):
-                for side, j in enumerate(self.pair(sign, i)):
-                    for field in range(2):
-                        yield sign, i, side, j, field, 4 * (sign * self.quad + i) + 2 * side + field
+    def tiles(self, sign):
+        for i in range(self.quad):
+            for side, j in enumerate(self.pair(sign, i)):
+                for field in range(2):
+                    yield i, side, j, field, 4 * i + 2 * side + field
 
 
 def iotas(plan):
@@ -168,11 +166,12 @@
     def part(at, _):
         packed = [[jnp.zeros(plan.tile, f32) for _ in range(2)] for _ in range(2)]
         for n in range(plan.group):
-            for sign, i, side, j, field, _ in plan.tiles():
-                slot = n * plan.half + sign * plan.quad + i
-                shift = 2 * slot - (lanes - 2 if side == 0 else 0)
-                value = rotate((f_ref, g_ref)[field][at * plan.group + n, j], shift, 1)
-                packed[side][field] = jnp.where(pair_lane == slot, value, packed[side][field])
+            for sign in range(2):
+                for i, side, j, field, _ in plan.tiles(sign):
+                    slot = n * plan.half + sign * plan.quad + i
+                    shift = 2 * slot - (lanes - 2 if side == 0 else 0)
+                    value = rotate((f_ref, g_ref)[field][at * plan.group + n, j], shift, 1)
+                    packed[side][field] = jnp.where(pair_lane == slot, value, packed[side][field])
         for side in range(2):
             for field in range(2):
                 where = field * plan.groups + at
@@ -215,27 +214,32 @@
     speed = jnp.where(in_group == 0, speeds[0], jnp.where(in_group == 1, speeds[1], speeds[2]))
     ua, va = (speed * weight for weight in lane_table)
     stay = 1.0 - ua - va
+
+    def along(x, below, above):
+        return jnp.where(
+            northward,
+            jnp.where(sub == 0, below, rotate(x, 1, 0)),
+            jnp.where(sub == rows - 1, above, rotate(x, -1, 0)),
+        )
+
     for side in range(2):
-        near, corner_masks = sides[side]
+        near, own, inner, corner_masks = sides[side]
         for field in range(2):
             here = here_at(side, field)
             below, above = (spread(corner_at(sign, side, field), plan) for sign in range(2))
             across = rotate(here, 1 if side == 0 else -1, 1)
-            along = jnp.where(
-                northward,
-                jnp.where(sub == 0, below, rotate(here, 1, 0)),
-                jnp.where(sub == rows - 1, above, rotate(here, -1, 0)),
-            )
-            after = near * (stay * here + ua * across + va * along)
-            corner = jnp.where(northward, corner_masks[0] * below, corner_masks[1] * above)
-            after = after + va * corner
+            after = near * (stay * here + ua * across + va * along(here, below, above))
+            after = after + va * jnp.where(northward, corner_masks[0] * below, corner_masks[1] * above)
+            once = own * (ua * here)
+            outer = own * (stay * once + ua * after + va * along(once, 0.0, 0.0))
+            second = inner * (ua * once)
             if side == 0:
-                out_at(side, field, jnp.where(odd, here, rotate(after, -1, 1)))
+                out_at(side, field, jnp.where(odd, second, rotate(outer, -1, 1)))
             else:
-                out_at(side, field, jnp.where(odd, rotate(after, 1, 1), here))
-
-
-def side_masks(plan, row_masks, col_ref):
+                out_at(side, field, jnp.where(odd, rotate(outer, 1, 1), second))
+
+
+def side_masks(plan, mask_ref, row_masks, col_ref):
     sub, _ = iotas(plan)
     rows, lanes = plan.tile
     sides = []
@@ -247,82 +251,107 @@
             jnp.where(sub == (0, rows - 1)[sign], spread(row_masks[sign][0:1, own : own + 1], plan), 0.0)
             for sign in range(2)
         ]
-        sides.append((near, corners))
+        mine = [
+            spread(mask_ref[:, at : at + 1].astype(f32), plan) for at in (own, own + (1 if side == 0 else -1))
+        ]
+        sides.append((near, *mine, corners))
     return sides
 
 
-def sweep(plan, count, mask, row_masks, weight_at, field_at, halo_at, column_at, store, scratch):
-    rows_after, *rest = scratch
-    columns_ref, first_ref, after_ref, second_ref = (rest[n * STAGES : (n + 1) * STAGES] for n in range(4))
+INTO = (1, -1)
+
+
+def weights(plan, weight_ref, level, i):
+    return [spread(weight_ref[level, t, row : row + 1, :], plan) for t, row in (divmod(3 * i + c, plan.rows) for c in range(3))]
+
+
+def inside(plan, count, mask, weight_ref, level_of, field_at, ext_ref, scratch):
+    moved_ref, after_ref, second_ref = (scratch[2 * n : 2 * n + 2] for n in range(3))
+    sub, lane = iotas(plan)
+    rows, lanes = plan.tile
+    edge_row, step_row, near_lane = (0, rows - 1), (1, -1), (0, lanes - 1)
+
+    def step(k, sign, value_at, moved_at):
+        for i, side, j, field, at in plan.tiles(sign):
+            stay, u, v = weights(plan, weight_ref, level_of(k), i)
+            u = jnp.where(lane == near_lane[side], 0.0, u)
+            v = jnp.where(sub == edge_row[sign], 0.0, v)
+            x = value_at(i, side, j, field, at)
+            yield side, j, field, at, mask * (stay * x + u * moved_at[at] + v * rotate(x, step_row[sign], 0))
+
+    def gather(k, sign):
+        for i, side, j, field, at in plan.tiles(sign):
+            moved_ref[sign][at] = rotate(field_at(field, k, j), INTO[side], 1)
+
+    def first(k, sign):
+        for side, j, field, at, x in step(k, sign, lambda i, side, j, field, at: field_at(field, k, j), moved_ref[sign]):
+            after_ref[sign][at] = x
+            second_ref[sign][at] = rotate(x, INTO[side], 1)
+
+    def second(k, sign):
+        for side, j, field, at, x in step(k, sign, lambda i, side, j, field, at: after_ref[sign][at], second_ref[sign]):
+            ext_ref[field, level_of(k) * plan.nd + j] = x
+
+    def turn(k, _):
+        before, here = jnp.maximum(k - 1, 0), jnp.minimum(k, count - 1)
+        second(before, 0)
+        first(before, 1)
+        gather(here, 0)
+        second(before, 1)
+        first(here, 0)
+        gather(here, 1)
+        return 0
+
+    lax.fori_loop(0, count + 1, turn, 0)
+
+
+def add_edges(plan, levels, mask_ref, row_masks, weight_ref, level_of, halo_at, column_at, ext_ref):
     sub, lane = iotas(plan)
     rows, lanes = plan.tile
     first_half = sub < rows // 2
     outer = (first_half & (lane == 0)) | (~first_half & (lane == lanes - 1))
-    edge_row, step_row = (0, rows - 1), (1, -1)
-    near_lane, into = (0, lanes - 1), (1, -1)
-
-    def weights(k, i):
-        return [spread(weight_at(k, *divmod(3 * i + c, rows)), plan) for c in range(3)]
-
-    def beside(x, halo, sign, side, field):
-        inner = 4 * side + 2 * field + 1 - sign
-        return jnp.where(sub == edge_row[sign], spread(halo(inner), plan), rotate(x, step_row[sign], 0))
-
-    def gather(k, slot):
+    odd = sub % 2 == 1
+
+    def sideways(x):
+        return jnp.where(outer, 0.0, jnp.where(first_half, rotate(x, 1, 1), rotate(x, -1, 1)))
+
+    edge, inner, beside = [], [], []
+    for sign in range(2):
+        at = 0 if sign == 0 else rows - 1
+        step = 1 if sign == 0 else -1
+        edge.append(spread(mask_ref[at : at + 1, :].astype(f32), plan))
+        inner.append(spread(mask_ref[at + step : at + step + 1, :].astype(f32), plan))
+        beside.append(sideways(edge[sign]))
+    for k in levels:
+        level = level_of(k)
         columns = [[column_at(k, side, field) for field in range(2)] for side in range(2)]
-        for sign, i, side, j, field, at in plan.tiles():
-            lane_at = 2 * (sign * plan.quad + i)
-            shift = -(lane_at + 1) if side == 0 else lanes - 1 - lane_at
-            column = rotate(columns[side][field], shift, 1)
-            columns_ref[slot][at] = column
-            moved = rotate(field_at(field, k, j), into[side], 1)
-            first_ref[slot][at] = jnp.where(lane == near_lane[side], column, moved)
-        for i in range(plan.quad):
-            stay, u, v = weights(k, i)
-            for sign in range(2):
-                halo = halo_at(sign, k, i)[...]
-                across = jnp.where(first_half, rotate(halo, 1, 1), rotate(halo, -1, 1))
-                across = jnp.where(outer, 0.0, across)
-                along = rotate(halo, step_row[sign], 0)
-                rows_after[sign, k * plan.quad + i] = row_masks[sign] * (stay * halo + u * across + v * along)
-
-    def first(k, slot):
-        for sign, i, side, j, field, at in plan.tiles():
-            stay, u, v = weights(k, i)
-            x = field_at(field, k, j)
-            halo = halo_at(sign, k, i)
-            y = beside(x, lambda n: halo[n : n + 1, :], sign, side, field)
-            x = mask * (stay * x + u * first_ref[slot][at] + v * y)
-            after_ref[slot][at] = x
-            far = lanes - 1 - near_lane[side]
-            second_ref[slot][at] = rotate(jnp.where(lane == far, columns_ref[slot][at], x), into[side], 1)
-
-    def second(k, slot):
-        for sign, i, side, j, field, at in plan.tiles():
-            stay, u, v = weights(k, i)
-            x = after_ref[slot][at]
-            halo = rows_after.at[sign, k * plan.quad + i]
-            y = beside(x, lambda n: halo[n : n + 1, :], sign, side, field)
-            store(field, k, j, mask * (stay * x + u * second_ref[slot][at] + v * y))
-
-    def clamp(k):
-        return jnp.clip(k, 0, count - 1)
-
-    def turn(t, _):
-        for n in range(STAGES):
-            at = t * STAGES + n
-            second(clamp(at - 2), (n - 2) % STAGES)
-            first(clamp(at - 1), (n - 1) % STAGES)
-            gather(clamp(at), n)
-        return 0
-
-    lax.fori_loop(0, -(-(count + 2) // STAGES), turn, 0)
-
-
-def sweep_scratch(plan, count):
-    return [pltpu.VMEM((2, count * plan.quad) + plan.tile, f32)] + [
-        pltpu.VMEM((2 * plan.nd,) + plan.tile, f32)
-    ] * (4 * STAGES)
+        for sign in range(2):
+            place = odd if sign == 0 else ~odd
+            for i in range(plan.quad):
+                stay, u, v = weights(plan, weight_ref, level, i)
+                halo = halo_at(sign, k, i)
+                nearest = jnp.where(place, halo, rotate(halo, -1 if sign == 0 else 1, 0))
+                shifted = sideways(nearest)
+                after = row_masks[sign] * (stay * nearest + u * shifted + v * halo)
+                once = edge[sign] * (v * nearest)
+                new = edge[sign] * (stay * once + u * (v * (beside[sign] * shifted)) + v * after)
+                new = jnp.where(place, inner[sign] * (v * once), new)
+                for side, j in enumerate(plan.pair(sign, i)):
+                    for field in range(2):
+                        n = 4 * side + 2 * field
+                        row_part = rotate(new, -n if sign == 0 else rows - 2 - n, 0)
+                        row_here = sub < 2 if sign == 0 else sub >= rows - 2
+                        slot = 2 * (sign * plan.quad + i)
+                        column = rotate(columns[side][field], -slot if side == 0 else lanes - 2 - slot, 1)
+                        lane_here = lane < 2 if side == 0 else lane >= lanes - 2
+                        at = level * plan.nd + j
+                        x = ext_ref[field, at]
+                        x = x + jnp.where(row_here, row_part, 0.0)
+                        ext_ref[field, at] = x + jnp.where(lane_here, column, 0.0)
+
+
+def half_scratch(plan):
+    return [pltpu.VMEM((plan.nd,) + plan.tile, f32)] * 6
 
 
 def halo_masks(plan, rows_ref):
@@ -330,19 +359,22 @@
     return [spread(rows_ref[0, plan.last, rows - 1 : rows, :], plan), spread(rows_ref[1, plan.last, 0:1, :], plan)]
 
 
-def turned(plan, tile, place):
-    back = lax.rem(plan.lanes - place * plan.nd, plan.lanes)
-    return pltpu.roll(tile, back, 1)
-
-
-def own_kernel(plan, bands, f_ref, g_ref, mask_ref, rows_ref, col_ref, corner_ref, weight_ref, ext_ref, both_ref, *scratch):
+def own_kernel(plan, f_ref, g_ref, mask_ref, weight_ref, ext_ref, *scratch):
+    mask = mask_ref[...].astype(f32)
+    inside(
+        plan, plan.bins, mask, weight_ref, lambda k: FH + k, lambda field, k, j: (f_ref, g_ref)[field][k, j],
+        ext_ref, scratch,
+    )
+
+
+def own_edges_kernel(plan, bands, mask_ref, rows_ref, col_ref, corner_ref, weight_ref, ext_in, ext_ref, column_ref):
     row_masks = halo_masks(plan, rows_ref)
-    sides = side_masks(plan, row_masks, col_ref)
+    sides = side_masks(plan, mask_ref, row_masks, col_ref)
     lane_table = lane_weights(plan)
     for part in range(plan.groups):
 
         def put(side, field, value):
-            both_ref[side, field, part] = value
+            column_ref[side, field, part] = value
 
         side_columns(
             plan, [level_speed(plan, bands, part * plan.group + n) for n in range(plan.group)], sides, lane_table,
@@ -351,36 +383,42 @@
             put,
         )
 
-    def store(field, k, j, value):
-        ext_ref[field, (FH + k) * plan.nd + j] = value
-
-    sweep(
-        plan, plan.bins, mask_ref[...].astype(f32), row_masks,
-        lambda k, t, row: weight_ref[FH + k, t, row : row + 1, :],
-        lambda field, k, j: (f_ref, g_ref)[field][k, j],
-        lambda sign, k, i: rows_ref.at[sign, k * plan.quad + i],
-        lambda k, side, field: turned(plan, both_ref[side, field, lax.div(k, plan.group)], lax.rem(k, plan.group)),
-        store, scratch,
-    )
-
-
-def halo_kernel(
-    plan, bands, raw_even, raw_odd, fwd_even, fwd_odd, mask_ref, rows_ref, col_ref, weight_ref, ext_in,
-    ext_ref, raw_ref, fwd_ref, both_ref, *scratch,
+    def part(at, _):
+        add_edges(
+            plan, range(plan.group), mask_ref, row_masks, weight_ref,
+            lambda n: FH + at * plan.group + n,
+            lambda sign, n, i: rows_ref[sign, (at * plan.group + n) * plan.quad + i],
+            lambda n, side, field: rotate(column_ref[side, field, at], -n * plan.nd, 1),
+            ext_ref,
+        )
+        return 0
+
+    lax.fori_loop(0, plan.groups, part, 0)
+
+
+def halo_kernel(plan, raw_even, raw_odd, mask_ref, weight_ref, ext_in, ext_ref, *scratch):
+    band = band_parity()
+    mask = mask_ref[...].astype(f32)
+    for above, ref in ((1 - band, raw_even), (band, raw_odd)):
+        start = above * (FH + plan.bins)
+        inside(
+            plan, FH, mask, weight_ref, lambda k: start + k, lambda field, k, j: ref[field, k, j], ext_ref, scratch
+        )
+
+
+def halo_edges_kernel(
+    plan, bands, fwd_even, fwd_odd, mask_ref, rows_ref, col_ref, weight_ref, ext_in, ext_ref, fwd_ref, column_ref
 ):
     band = band_parity()
-    for field in range(2):
-        raw_ref[field, pl.ds((1 - band) * FH, FH)] = raw_even[field]
-        raw_ref[field, pl.ds(band * FH, FH)] = raw_odd[field]
     fwd_ref[1 - band] = fwd_even[...]
     fwd_ref[band] = fwd_odd[...]
     row_masks = halo_masks(plan, rows_ref)
-    sides = side_masks(plan, row_masks, col_ref)
+    sides = side_masks(plan, mask_ref, row_masks, col_ref)
     lane_table = lane_weights(plan)
     for part in range(2):
 
         def put(side, field, value):
-            both_ref[side, field, part] = value
+            column_ref[side, field, part] = value
 
         def corner(sign, side, field):
             row = 4 * sign + 2 * side + field
@@ -393,26 +431,17 @@
             put,
         )
 
-    def level(k):
-        return jnp.where(k < FH, k, k + plan.bins)
-
-    def store(field, k, j, value):
-        ext_ref[field, level(k) * plan.nd + j] = value
-
-    def halo(sign, k, i):
-        part = jnp.where(k < FH, 0, 1)
-        return fwd_ref.at[part, sign * plan.sent_rows + (k - part * FH) * plan.quad + i]
-
-    def column(k, side, field):
-        part = jnp.where(k < FH, 0, 1)
-        return turned(plan, both_ref[side, field, part], k - part * FH)
-
-    sweep(
-        plan, 2 * FH, mask_ref[...].astype(f32), row_masks,
-        lambda k, t, row: weight_ref[level(k), t, row : row + 1, :],
-        lambda field, k, j: raw_ref[field, k, j],
-        halo, column, store, scratch,
-    )
+    def part(at, _):
+        add_edges(
+            plan, range(FH), mask_ref, row_masks, weight_ref,
+            lambda n: at * (FH + plan.bins) + n,
+            lambda sign, n, i: fwd_ref[at, sign * plan.sent_rows + n * plan.quad + i],
+            lambda n, side, field: rotate(column_ref[side, field, at], -n * plan.nd, 1),
+            ext_ref,
+        )
+        return 0
+
+    lax.fori_loop(0, 2, part, 0)
 
 
 def source_levels(plan, freq_ref, dir_ref, coupling_ref, ext_ref, fo_ref, go_ref, first, last):
@@ -454,7 +483,7 @@
             out_g[n] = g0 - strength * change
         return 0
 
-    lax.fori_loop(first, last, direction, 0)
+    lax.fori_loop(first, last, direction, 0, unroll=2)
 
 
 def flat(plan, ref):
@@ -560,6 +589,7 @@
         cols = sideways(cols, None)
         corner_odd = sideways(corner_odd, 1)
         corner_even = sideways(corner_even, 0)
+        (ext,) = kernel(own_kernel, (ext_out,), [VM] * 4, half_scratch(plan))(f, g, mask, weights)
         sorted_out = (array(2, plan.last + 1), jax.ShapeDtypeStruct((2,) + corner_out.shape, f32), fwd_out, fwd_out)
         halo_rows, corners, fwd_even, fwd_odd = kernel(forward_kernel, sorted_out, [VM] * 5)(
             even, odd, cols, corner_even, corner_odd
@@ -567,17 +597,19 @@
         fwd_odd = band_swap(fwd_odd, 1)
         fwd_even = band_swap(fwd_even, 0)
         (ext,) = kernel(
-            own_kernel, (ext_out,), [VM] * 7, [both] + sweep_scratch(plan, bins), static=(bands,)
-        )(f, g, mask, halo_rows, cols, corners, weights)
+            own_edges_kernel, (ext_out,), [VM] * 6, [both], aliases={5: 0}, static=(bands,)
+        )(mask, halo_rows, cols, corners, weights, ext)
+        (ext,) = kernel(halo_kernel, (ext_out,), [VM] * 5, half_scratch(plan), aliases={4: 0})(
+            raw_even, raw_odd, mask, weights, ext,
+        )
         (ext,) = kernel(
-            halo_kernel,
+            halo_edges_kernel,
             (ext_out,),
-            [VM] * 9,
-            [pltpu.VMEM((2, 2 * FH, nd) + plan.tile, f32), pltpu.VMEM((2, plan.sent) + plan.tile, f32), both]
-            + sweep_scratch(plan, 2 * FH),
-            aliases={8: 0},
+            [VM] * 7,
+            [pltpu.VMEM((2, plan.sent) + plan.tile, f32), both],
+            aliases={6: 0},
             static=(bands,),
-        )(raw_even, raw_odd, fwd_even, fwd_odd, mask, halo_rows, cols, weights, ext)
+        )(fwd_even, fwd_odd, mask, halo_rows, cols, weights, ext)
         if step < STEPS - 1:
             f, g, even, odd, raw_even, raw_odd = kernel(
                 source_kernel, (field, field, row_out, row_out, raw_out, raw_out), [SM] * 3 + [VM] * 2, [sorted_rows]

time: 94.5 us -> 91.3 us (0.966)
  Pallas kernels: 30.3 us -> 27.1 us
    pallas_call x4 -> x8, Pallas kernels: 18.7 us -> 16.2 us  [the longest x2 5.46 us: body(): kernel(own_kernel, (ext_out,), [VM] * 4, half_scratch(plan))]
  transfers between devices with their start and end apart: 18 -> 18, of which waited for: 7 -> 6; matrix products, arithmetic and copies ran while one was open for 0% -> 0% of each run, Pallas kernels for 14% -> 17%
where the time goes in v1:
time: 91.3 us; the launch traced here: 90.9 us
  starting transfers between devices  33.7 us (37%)
  waiting for transfers between devices  28.3 us (31%)
  Pallas kernels  27.1 us (30%)
  between operations  0.96 us (1%)
    ppermute x6, waiting for transfers between devices, sideways(): return lax.ppermute(value, 'tile', tile_pairs(parity, 1))  28.3 us
    ppermute x8, starting transfers between devices, band_swap(): lax.ppermute(value, 'band', [(a, b) for a, b in pairs if 0 <= b < bands])  15.6 us
    ppermute x4, starting transfers between devices, tile_swap(): return lax.ppermute(value, 'tile', tile_pairs(parity, 0))  11.7 us
    ppermute x6, starting transfers between devices, sideways(): return lax.ppermute(value, 'tile', tile_pairs(parity, 1))  6.37 us
    pallas_call x2, Pallas kernels, body(): kernel(own_kernel, (ext_out,), [VM] * 4, half_scratch(plan))  5.46 us
    pallas_call x2, Pallas kernels, body(): kernel(halo_kernel, (ext_out,), [VM] * 5, half_scratch(plan), aliases={4:...  4.42 us
    pallas_call x2, Pallas kernels, body(): kernel(own_edges_kernel, (ext_out,), [VM] * 6, [both], aliases={5: 0}, st...  3.7 us
    pallas_call x1, Pallas kernels, body(): kernel(lambda plan, *refs: last_kernel(plan, chunks, *refs), (field, fiel...  3.49 us
  transfers between devices with their start and end apart: 18, of which 6 were waited for; matrix products, arithmetic and copies ran while one was open for 0% of the time, Pallas kernels for 17%

profile of v1, /device:TPU:1, one launch (start us, length us, event | category | flops | bytes accessed | tf_op | source)
XLA Modules:
  0.0 90.9 jit_solution(15695125248395400933)
XLA Ops:
  0.6 0.7 copy-done
  1.4 2.3 %shard_map.77 = (f32[9,36,8,128]{3,2,1,0:T(8,128)S(1)}, f32[9,36,8,128]{3,2,1,0:T(8,128)S(1)}, f32[82,8,128]{2,1,0:T(8,128)S(1)}, f32[82,8,128]{2,1,0:T(8,128)S(...) custom-call(f32[9,36,8,128]{3,2,1,0:T(8,128)} %bitcast.21, ...), custom_call_target="tpu_custom_call" | custom-call | tf_op jit(solution)/shard_map/pallas_call | solution.py:575
  3.8 4.5 %collective-permute-start.8 = (f32[2,3,36,8,128]{4,3,2,1,0:T(8,128)S(1)}, f32[2,3,36,8,128]{4,3,2,1,0:T(8,128)S(1)}, u32[]{:S(2)}, u32[]{:S(2)}) collective-permute-start(f32[2,3,36,8,128]{4,3,2,1,0:T(8,128)S(1)} %get-tuple-element.43), channel_id=1, source_target_pairs={{1,2},{2,1},{5,6},{6,5},{9,10},{10,9},{13,14},{14,13},{17,18},{18,... | collective-permute-start | bytes 2654216 | tf_op jit(solution)/shard_map/ppermute | solution.py:573
  8.3 1.3 %collective-permute-start = (f32[82,8,128]{2,1,0:T(8,128)S(1)}, f32[82,8,128]{2,1,0:T(8,128)S(1)}, u32[]{:S(2)}, u32[]{:S(2)}) collective-permute-start(f32[82,8,128]{2,1,0:T(8,128)S(1)} %get-tuple-element.31), channel_id=1, source_target_pairs={{0,4},{4,0},{8,12},{12,8},{16,20},{20,16},{24,28},{28,24},{1,5},{5... | collective-permute-start | bytes 1007624 | tf_op jit(solution)/shard_map/ppermute | solution.py:562
  9.6 5.2 %collective-permute-start.1 = (f32[82,8,128]{2,1,0:T(8,128)S(1)}, f32[82,8,128]{2,1,0:T(8,128)S(1)}, u32[]{:S(2)}, u32[]{:S(2)}) collective-permute-start(f32[82,8,128]{2,1,0:T(8,128)S(1)} %get-tuple-element.32), channel_id=1, source_target_pairs={{0,28},{12,16},{16,12},{28,0},{1,29},{13,17},{17,13},{29,1},{2,30}... | collective-permute-start | bytes 1007624 | tf_op jit(solution)/shard_map/ppermute | solution.py:562
  14.8 0.9 shard_map.78
  15.8 6.8 %collective-permute-done.3.corner_even = f32[2,8,128]{2,1,0:T(8,128)S(1)} collective-permute-done((f32[2,8,128]{2,1,0:T(8,128)S(1)}, f32[2,8,128]{2,1,0:T(8,128)S(1)}, u32[]{:S(2)}, u32[]{:S(2)}) %collective-permute-start.3) | collective-permute-done | bytes 8224 | tf_op jit(solution)/shard_map/ppermute | solution.py:566
  22.6 1.9 %collective-permute-start.4 = (f32[2,8,128]{2,1,0:T(8,128)S(1)}, f32[2,8,128]{2,1,0:T(8,128)S(1)}, u32[]{:S(2)}, u32[]{:S(2)}) collective-permute-start(f32[2,8,128]{2,1,0:T(8,128)S(1)} %get-tuple-element.37), channel_id=1, source_target_pairs={{0,12},{12,0},{16,28},{28,16},{1,13},{13,1},{17,29},{29,17},{2,14}... | collective-permute-start | bytes 24584 | tf_op jit(solution)/shard_map/ppermute | solution.py:566
  24.5 3.4 %collective-permute-done.4.corner_odd = f32[2,8,128]{2,1,0:T(8,128)S(1)} collective-permute-done((f32[2,8,128]{2,1,0:T(8,128)S(1)}, f32[2,8,128]{2,1,0:T(8,128)S(1)}, u32[]{:S(2)}, u32[]{:S(2)}) %collective-permute-start.4) | collective-permute-done | bytes 8224 | tf_op jit(solution)/shard_map/ppermute | solution.py:566
  27.9 1.2 %collective-permute-start.2 = (f32[2,7,8,128]{3,2,1,0:T(8,128)S(1)}, f32[2,7,8,128]{3,2,1,0:T(8,128)S(1)}, u32[]{:S(2)}, u32[]{:S(2)}) collective-permute-start(f32[2,7,8,128]{3,2,1,0:T(8,128)S(1)} %get-tuple-element.35), channel_id=1, source_target_pairs={{0,16},{4,20},{8,24},{12,28},{16,0},{20,4},{24,8},{28,12},{1,17},{... | collective-permute-start | bytes 172040 | tf_op jit(solution)/shard_map/ppermute | solution.py:566
  29.1 3.6 %collective-permute-done.2.col_ref = f32[2,7,8,128]{3,2,1,0:T(8,128)S(1)} collective-permute-done((f32[2,7,8,128]{3,2,1,0:T(8,128)S(1)}, f32[2,7,8,128]{3,2,1,0:T(8,128)S(1)}, u32[]{:S(2)}, u32[]{:S(2)}) %collective-permute-start.2) | collective-permute-done | bytes 57376 | tf_op jit(solution)/shard_map/ppermute | solution.py:566
  33.3 3.9 %collective-permute-start.6 = (f32[59,8,128]{2,1,0:T(8,128)S(1)}, f32[59,8,128]{2,1,0:T(8,128)S(1)}, u32[]{:S(2)}, u32[]{:S(2)}) collective-permute-start(f32[59,8,128]{2,1,0:T(8,128)S(1)} %get-tuple-element.39), channel_id=1, source_target_pairs={{1,2},{2,1},{5,6},{6,5},{9,10},{10,9},{13,14},{14,13},{17,18},{18,... | collective-permute-start | bytes 725000 | tf_op jit(solution)/shard_map/ppermute | solution.py:573
  37.2 2.7 %shard_map.80.ext_in = f32[2,540,8,128]{3,2,1,0:T(8,128)S(1)} custom-call(f32[9,36,8,128]{3,2,1,0:T(8,128)S(1)} %get-tuple-element.33.f_ref, f32[9,36,8,128]{3,2,1,0:T(8,128)S(1)} %get-tuple-element.34.g_ref, s32[8,128]{1,0:T(8,128)S(1)} %bitcast.11, f32[15,4,8,128]{3,2,1,0:T(8,128)S(1)} %get-tuple-element.41.weight_ref), custom_call_target="tpu_custom_call" | custom-call | tf_op jit(solution)/shard_map/pallas_call | solution.py:592
  40.0 1.8 %shard_map.81.ext_in = f32[2,540,8,128]{3,2,1,0:T(8,128)S(1)} custom-call(s32[8,128]{1,0:T(8,128)S(1)} %bitcast.12, f32[2,82,8,128]{3,2,1,0:T(8,128)S(1)} %get-tuple-element.40.rows_ref, f32[2,7,8,128]{3,2,1,0:T(8,128)S(1)} %collective-permute-done.2.col_ref, f32[2,2,8,128]{3,2,1,0:T(8,128)S(1)} %get-tuple-element.44.corner_ref, ...), custom_call_target="tpu_custom_call", output_to_operand_aliasing={{}: (5, {})} | custom-call | tf_op jit(solution)/shard_map/pallas_call | solution.py:599
  41.9 2.2 %shard_map.82.ext_in = f32[2,540,8,128]{3,2,1,0:T(8,128)S(1)} custom-call(f32[2,3,36,8,128]{4,3,2,1,0:T(8,128)S(1)} %collective-permute-done.7.raw_even, f32[2,3,36,8,128]{4,3,2,1,0:T(8,128)S(1)} %collective-permute-done.8.raw_odd, s32[8,128]{1,0:T(8,128)S(1)} %bitcast.13, ...), custom_call_target="tpu_custom_call", output_to_operand_aliasing={{}: (4, {})} | custom-call | tf_op jit(solution)/shard_map/pallas_call | solution.py:602
  44.2 1.3 %shard_map.83.ext_ref = f32[2,540,8,128]{3,2,1,0:T(8,128)S(1)} custom-call(f32[59,8,128]{2,1,0:T(8,128)S(1)} %collective-permute-done.5.fwd_even, f32[59,8,128]{2,1,0:T(8,128)S(1)} %collective-permute-done.6.fwd_odd, s32[8,128]{1,0:T(8,128)S(1)} %bitcast.14, f32[2,82,8,128]{3,2,1,0:T(8,128)S(1)} %get-tuple-element.40.rows_ref, ...), custom_call_target="tpu_custom_call", output_to_operand_aliasing={{}: (6, {})} | custom-call | tf_op jit(solution)/shard_map/pallas_call | solution.py:605
  45.5 3.0 %shard_map.84 = (f32[9,36,8,128]{3,2,1,0:T(8,128)S(1)}, f32[9,36,8,128]{3,2,1,0:T(8,128)S(1)}, f32[82,8,128]{2,1,0:T(8,128)S(1)}, f32[82,8,128]{2,1,0:T(8,128)S(...) custom-call(s32[2]{0:T(128)S(1)} %copy-done.2, s32[2]{0:T(128)S(1)} %copy-done.3, ...), custom_call_target="tpu_custom_call" | custom-call | tf_op jit(solution)/shard_map/pallas_call | solution.py:614
  48.6 1.9 %collective-permute-start.17 = (f32[2,3,36,8,128]{4,3,2,1,0:T(8,128)S(1)}, f32[2,3,36,8,128]{4,3,2,1,0:T(8,128)S(1)}, u32[]{:S(2)}, u32[]{:S(2)}) collective-permute-start(f32[2,3,36,8,128]{4,3,2,1,0:T(8,128)S(1)} %get-tuple-element.56), channel_id=1, source_target_pairs={{1,2},{2,1},{5,6},{6,5},{9,10},{10,9},{13,14},{14,13},{17,18},{18,... | collective-permute-start | bytes 2654216 | tf_op jit(solution)/shard_map/ppermute | solution.py:573
  50.6 5.2 %collective-permute-start.10 = (f32[82,8,128]{2,1,0:T(8,128)S(1)}, f32[82,8,128]{2,1,0:T(8,128)S(1)}, u32[]{:S(2)}, u32[]{:S(2)}) collective-permute-start(f32[82,8,128]{2,1,0:T(8,128)S(1)} %get-tuple-element.46), channel_id=1, source_target_pairs={{0,28},{12,16},{16,12},{28,0},{1,29},{13,17},{17,13},{29,1},{2,30}... | collective-permute-start | bytes 1007624 | tf_op jit(solution)/shard_map/ppermute | solution.py:562
  55.8 0.9 %shard_map.85 = (f32[2,7,8,128]{3,2,1,0:T(8,128)S(1)}, f32[2,8,128]{2,1,0:T(8,128)S(1)}, f32[2,8,128]{2,1,0:T(8,128)S(1)}) custom-call(f32[9,36,8,128]{3,2,1,0:T(8,128)S(1)} %get-tuple-element.47.f_ref, f32[9,36,8,128]{3,2,1,0:T(8,128)S(1)} %get-tuple-element.48.g_ref, s32[8,128]{1,0:T(8,128)S(1)} %bitcast.16), custom_call_target="tpu_custom_call" | custom-call | tf_op jit(solution)/shard_map/pallas_call | solution.py:588
  56.8 8.4 %collective-permute-done.12.corner_even = f32[2,8,128]{2,1,0:T(8,128)S(1)} collective-permute-done((f32[2,8,128]{2,1,0:T(8,128)S(1)}, f32[2,8,128]{2,1,0:T(8,128)S(1)}, u32[]{:S(2)}, u32[]{:S(2)}) %collective-permute-start.12) | collective-permute-done | bytes 8224 | tf_op jit(solution)/shard_map/ppermute | solution.py:566
  65.2 1.9 %collective-permute-start.13 = (f32[2,8,128]{2,1,0:T(8,128)S(1)}, f32[2,8,128]{2,1,0:T(8,128)S(1)}, u32[]{:S(2)}, u32[]{:S(2)}) collective-permute-start(f32[2,8,128]{2,1,0:T(8,128)S(1)} %get-tuple-element.51), channel_id=1, source_target_pairs={{0,12},{12,0},{16,28},{28,16},{1,13},{13,1},{17,29},{29,17},{2,14}... | collective-permute-start | bytes 24584 | tf_op jit(solution)/shard_map/ppermute | solution.py:566
  67.1 3.4 %collective-permute-done.13.corner_odd = f32[2,8,128]{2,1,0:T(8,128)S(1)} collective-permute-done((f32[2,8,128]{2,1,0:T(8,128)S(1)}, f32[2,8,128]{2,1,0:T(8,128)S(1)}, u32[]{:S(2)}, u32[]{:S(2)}) %collective-permute-start.13) | collective-permute-done | bytes 8224 | tf_op jit(solution)/shard_map/ppermute | solution.py:566
  70.5 1.2 %collective-permute-start.11 = (f32[2,7,8,128]{3,2,1,0:T(8,128)S(1)}, f32[2,7,8,128]{3,2,1,0:T(8,128)S(1)}, u32[]{:S(2)}, u32[]{:S(2)}) collective-permute-start(f32[2,7,8,128]{3,2,1,0:T(8,128)S(1)} %get-tuple-element.49), channel_id=1, source_target_pairs={{0,16},{4,20},{8,24},{12,28},{16,0},{20,4},{24,8},{28,12},{1,17},{... | collective-permute-start | bytes 172040 | tf_op jit(solution)/shard_map/ppermute | solution.py:566
  71.7 2.7 %collective-permute-done.11.col_ref = f32[2,7,8,128]{3,2,1,0:T(8,128)S(1)} collective-permute-done((f32[2,7,8,128]{3,2,1,0:T(8,128)S(1)}, f32[2,7,8,128]{3,2,1,0:T(8,128)S(1)}, u32[]{:S(2)}, u32[]{:S(2)}) %collective-permute-start.11) | collective-permute-done | bytes 57376 | tf_op jit(solution)/shard_map/ppermute | solution.py:566
  74.5 2.8 %collective-permute-start.14 = (f32[59,8,128]{2,1,0:T(8,128)S(1)}, f32[59,8,128]{2,1,0:T(8,128)S(1)}, u32[]{:S(2)}, u32[]{:S(2)}) collective-permute-start(f32[59,8,128]{2,1,0:T(8,128)S(1)} %get-tuple-element.52), channel_id=1, source_target_pairs={{0,1},{1,0},{2,3},{3,2},{4,5},{5,4},{6,7},{7,6},{8,9},{9,8},{10,11... | collective-permute-start | bytes 725000 | tf_op jit(solution)/shard_map/ppermute | solution.py:573
  77.3 1.9 %collective-permute-start.15 = (f32[59,8,128]{2,1,0:T(8,128)S(1)}, f32[59,8,128]{2,1,0:T(8,128)S(1)}, u32[]{:S(2)}, u32[]{:S(2)}) collective-permute-start(f32[59,8,128]{2,1,0:T(8,128)S(1)} %get-tuple-element.53), channel_id=1, source_target_pairs={{1,2},{2,1},{5,6},{6,5},{9,10},{10,9},{13,14},{14,13},{17,18},{18,... | collective-permute-start | bytes 725000 | tf_op jit(solution)/shard_map/ppermute | solution.py:573
  79.2 2.7 %shard_map.87.ext_in = f32[2,540,8,128]{3,2,1,0:T(8,128)S(1)} custom-call(f32[9,36,8,128]{3,2,1,0:T(8,128)S(1)} %get-tuple-element.47.f_ref, f32[9,36,8,128]{3,2,1,0:T(8,128)S(1)} %get-tuple-element.48.g_ref, s32[8,128]{1,0:T(8,128)S(1)} %bitcast.17, f32[15,4,8,128]{3,2,1,0:T(8,128)S(1)} %get-tuple-element.41.weight_ref), custom_call_target="tpu_custom_call" | custom-call | tf_op jit(solution)/shard_map/pallas_call | solution.py:592
  81.9 1.9 %shard_map.88.ext_in = f32[2,540,8,128]{3,2,1,0:T(8,128)S(1)} custom-call(s32[8,128]{1,0:T(8,128)S(1)} %bitcast.18, f32[2,82,8,128]{3,2,1,0:T(8,128)S(1)} %get-tuple-element.54.rows_ref, f32[2,7,8,128]{3,2,1,0:T(8,128)S(1)} %collective-permute-done.11.col_ref, f32[2,2,8,128]{3,2,1,0:T(8,128)S(1)} %get-tuple-element.57.corner_ref, ...), custom_call_target="tpu_custom_call", output_to_operand_aliasing={{}: (5, {})} | custom-call | tf_op jit(solution)/shard_map/pallas_call | solution.py:599
  83.8 2.2 %shard_map.89.ext_in = f32[2,540,8,128]{3,2,1,0:T(8,128)S(1)} custom-call(f32[2,3,36,8,128]{4,3,2,1,0:T(8,128)S(1)} %collective-permute-done.16.raw_even, f32[2,3,36,8,128]{4,3,2,1,0:T(8,128)S(1)} %collective-permute-done.17.raw_odd, s32[8,128]{1,0:T(8,128)S(1)} %bitcast.19, ...), custom_call_target="tpu_custom_call", output_to_operand_aliasing={{}: (4, {})} | custom-call | tf_op jit(solution)/shard_map/pallas_call | solution.py:602
  86.1 1.3 %shard_map.90.refs_3_ = f32[2,540,8,128]{3,2,1,0:T(8,128)S(1)} custom-call(f32[59,8,128]{2,1,0:T(8,128)S(1)} %collective-permute-done.14.fwd_even, f32[59,8,128]{2,1,0:T(8,128)S(1)} %collective-permute-done.15.fwd_odd, s32[8,128]{1,0:T(8,128)S(1)} %bitcast.20, f32[2,82,8,128]{3,2,1,0:T(8,128)S(1)} %get-tuple-element.54.rows_ref, ...), custom_call_target="tpu_custom_call", output_to_operand_aliasing={{}: (6, {})} | custom-call | tf_op jit(solution)/shard_map/pallas_call | solution.py:605
  87.4 3.5 %shard_map.91 = (f32[9,36,8,128]{3,2,1,0:T(8,128)}, f32[9,36,8,128]{3,2,1,0:T(8,128)}) custom-call(s32[2]{0:T(128)S(1)} %copy-done.2, s32[2]{0:T(128)S(1)} %copy-done.3, f32[9]{0:T(128)S(1)} %copy-done.4, f32[2,540,8,128]{3,2,1,0:T(8,128)S(1)} %shard_map.90.refs_3_), custom_call_target="tpu_custom_call" | custom-call | tf_op jit(solution)/shard_map/pallas_call | solution.py:619
  (29 shorter events, 1.1 us)
Async XLA Ops:
  0.6 36.6 %copy-start.1 = (s32[1,8,128]{2,1,0:T(8,128)S(1)}, s32[1,8,128]{2,1,0:T(8,128)}, u32[]{:S(2)}) copy-start(s32[1,8,128]{2,1,0:T(8,128)} %param.8) | copy-start | bytes 12292
  0.6 0.8 copy-start
  3.7 38.1 %collective-permute-start.7 = (f32[2,3,36,8,128]{4,3,2,1,0:T(8,128)S(1)}, f32[2,3,36,8,128]{4,3,2,1,0:T(8,128)S(1)}, u32[]{:S(2)}, u32[]{:S(2)}) collective-permute-start(f32[2,3,36,8,128]{4,3,2,1,0:T(8,128)S(1)} %get-tuple-element.42), channel_id=1, source_target_pairs={{0,1},{1,0},{2,3},{3,2},{4,5},{5,4},{6,7},{7,6},{8,9},{9,8},{10,11... | collective-permute-start | bytes 2654216 | tf_op jit(solution)/shard_map/ppermute | solution.py:573
  3.8 38.1 %collective-permute-start.8 = (f32[2,3,36,8,128]{4,3,2,1,0:T(8,128)S(1)}, f32[2,3,36,8,128]{4,3,2,1,0:T(8,128)S(1)}, u32[]{:S(2)}, u32[]{:S(2)}) collective-permute-start(f32[2,3,36,8,128]{4,3,2,1,0:T(8,128)S(1)} %get-tuple-element.43), channel_id=1, source_target_pairs={{1,2},{2,1},{5,6},{6,5},{9,10},{10,9},{13,14},{14,13},{17,18},{18,... | collective-permute-start | bytes 2654216 | tf_op jit(solution)/shard_map/ppermute | solution.py:573
  8.3 24.4 %collective-permute-start = (f32[82,8,128]{2,1,0:T(8,128)S(1)}, f32[82,8,128]{2,1,0:T(8,128)S(1)}, u32[]{:S(2)}, u32[]{:S(2)}) collective-permute-start(f32[82,8,128]{2,1,0:T(8,128)S(1)} %get-tuple-element.31), channel_id=1, source_target_pairs={{0,4},{4,0},{8,12},{12,8},{16,20},{20,16},{24,28},{28,24},{1,5},{5... | collective-permute-start | bytes 1007624 | tf_op jit(solution)/shard_map/ppermute | solution.py:562
  9.6 23.1 %collective-permute-start.1 = (f32[82,8,128]{2,1,0:T(8,128)S(1)}, f32[82,8,128]{2,1,0:T(8,128)S(1)}, u32[]{:S(2)}, u32[]{:S(2)}) collective-permute-start(f32[82,8,128]{2,1,0:T(8,128)S(1)} %get-tuple-element.32), channel_id=1, source_target_pairs={{0,28},{12,16},{16,12},{28,0},{1,29},{13,17},{17,13},{29,1},{2,30}... | collective-permute-start | bytes 1007624 | tf_op jit(solution)/shard_map/ppermute | solution.py:562
  15.7 6.9 %collective-permute-start.3 = (f32[2,8,128]{2,1,0:T(8,128)S(1)}, f32[2,8,128]{2,1,0:T(8,128)S(1)}, u32[]{:S(2)}, u32[]{:S(2)}) collective-permute-start(f32[2,8,128]{2,1,0:T(8,128)S(1)} %get-tuple-element.36), channel_id=1, source_target_pairs={{0,20},{4,16},{8,28},{12,24},{16,4},{20,0},{24,12},{28,8},{1,21},{... | collective-permute-start | bytes 24584 | tf_op jit(solution)/shard_map/ppermute | solution.py:566
  22.6 5.3 %collective-permute-start.4 = (f32[2,8,128]{2,1,0:T(8,128)S(1)}, f32[2,8,128]{2,1,0:T(8,128)S(1)}, u32[]{:S(2)}, u32[]{:S(2)}) collective-permute-start(f32[2,8,128]{2,1,0:T(8,128)S(1)} %get-tuple-element.37), channel_id=1, source_target_pairs={{0,12},{12,0},{16,28},{28,16},{1,13},{13,1},{17,29},{29,17},{2,14}... | collective-permute-start | bytes 24584 | tf_op jit(solution)/shard_map/ppermute | solution.py:566
  27.9 4.8 %collective-permute-start.2 = (f32[2,7,8,128]{3,2,1,0:T(8,128)S(1)}, f32[2,7,8,128]{3,2,1,0:T(8,128)S(1)}, u32[]{:S(2)}, u32[]{:S(2)}) collective-permute-start(f32[2,7,8,128]{3,2,1,0:T(8,128)S(1)} %get-tuple-element.35), channel_id=1, source_target_pairs={{0,16},{4,20},{8,24},{12,28},{16,0},{20,4},{24,8},{28,12},{1,17},{... | collective-permute-start | bytes 172040 | tf_op jit(solution)/shard_map/ppermute | solution.py:566
  32.8 11.3 %collective-permute-start.5 = (f32[59,8,128]{2,1,0:T(8,128)S(1)}, f32[59,8,128]{2,1,0:T(8,128)S(1)}, u32[]{:S(2)}, u32[]{:S(2)}) collective-permute-start(f32[59,8,128]{2,1,0:T(8,128)S(1)} %get-tuple-element.38), channel_id=1, source_target_pairs={{0,1},{1,0},{2,3},{3,2},{4,5},{5,4},{6,7},{7,6},{8,9},{9,8},{10,11... | collective-permute-start | bytes 725000 | tf_op jit(solution)/shard_map/ppermute | solution.py:573
  33.3 10.9 %collective-permute-start.6 = (f32[59,8,128]{2,1,0:T(8,128)S(1)}, f32[59,8,128]{2,1,0:T(8,128)S(1)}, u32[]{:S(2)}, u32[]{:S(2)}) collective-permute-start(f32[59,8,128]{2,1,0:T(8,128)S(1)} %get-tuple-element.39), channel_id=1, source_target_pairs={{1,2},{2,1},{5,6},{6,5},{9,10},{10,9},{13,14},{14,13},{17,18},{18,... | collective-permute-start | bytes 725000 | tf_op jit(solution)/shard_map/ppermute | solution.py:573
  44.1 1.4 %copy-start.2 = (s32[2]{0:T(128)S(1)}, s32[2]{0:T(128)}, u32[]{:S(2)}) copy-start(s32[2]{0:T(128)} %refs_0_.1) | copy-start | bytes 28
  44.1 1.4 %copy-start.3 = (s32[2]{0:T(128)S(1)}, s32[2]{0:T(128)}, u32[]{:S(2)}) copy-start(s32[2]{0:T(128)} %refs_1_.1) | copy-start | bytes 28
  44.1 1.4 %copy-start.4 = (f32[9]{0:T(128)S(1)}, f32[9]{0:T(128)}, u32[]{:S(2)}) copy-start(f32[9]{0:T(128)} %refs_2_.1) | copy-start | bytes 112
  48.5 35.3 %collective-permute-start.16 = (f32[2,3,36,8,128]{4,3,2,1,0:T(8,128)S(1)}, f32[2,3,36,8,128]{4,3,2,1,0:T(8,128)S(1)}, u32[]{:S(2)}, u32[]{:S(2)}) collective-permute-start(f32[2,3,36,8,128]{4,3,2,1,0:T(8,128)S(1)} %get-tuple-element.55), channel_id=1, source_target_pairs={{0,1},{1,0},{2,3},{3,2},{4,5},{5,4},{6,7},{7,6},{8,9},{9,8},{10,11... | collective-permute-start | bytes 2654216 | tf_op jit(solution)/shard_map/ppermute | solution.py:573
  48.6 35.2 %collective-permute-start.17 = (f32[2,3,36,8,128]{4,3,2,1,0:T(8,128)S(1)}, f32[2,3,36,8,128]{4,3,2,1,0:T(8,128)S(1)}, u32[]{:S(2)}, u32[]{:S(2)}) collective-permute-start(f32[2,3,36,8,128]{4,3,2,1,0:T(8,128)S(1)} %get-tuple-element.56), channel_id=1, source_target_pairs={{1,2},{2,1},{5,6},{6,5},{9,10},{10,9},{13,14},{14,13},{17,18},{18,... | collective-permute-start | bytes 2654216 | tf_op jit(solution)/shard_map/ppermute | solution.py:573
  50.6 23.9 %collective-permute-start.9 = (f32[82,8,128]{2,1,0:T(8,128)S(1)}, f32[82,8,128]{2,1,0:T(8,128)S(1)}, u32[]{:S(2)}, u32[]{:S(2)}) collective-permute-start(f32[82,8,128]{2,1,0:T(8,128)S(1)} %get-tuple-element.45), channel_id=1, source_target_pairs={{0,4},{4,0},{8,12},{12,8},{16,20},{20,16},{24,28},{28,24},{1,5},{5... | collective-permute-start | bytes 1007624 | tf_op jit(solution)/shard_map/ppermute | solution.py:562
  50.6 23.8 %collective-permute-start.10 = (f32[82,8,128]{2,1,0:T(8,128)S(1)}, f32[82,8,128]{2,1,0:T(8,128)S(1)}, u32[]{:S(2)}, u32[]{:S(2)}) collective-permute-start(f32[82,8,128]{2,1,0:T(8,128)S(1)} %get-tuple-element.46), channel_id=1, source_target_pairs={{0,28},{12,16},{16,12},{28,0},{1,29},{13,17},{17,13},{29,1},{2,30}... | collective-permute-start | bytes 1007624 | tf_op jit(solution)/shard_map/ppermute | solution.py:562
  56.7 8.5 %collective-permute-start.12 = (f32[2,8,128]{2,1,0:T(8,128)S(1)}, f32[2,8,128]{2,1,0:T(8,128)S(1)}, u32[]{:S(2)}, u32[]{:S(2)}) collective-permute-start(f32[2,8,128]{2,1,0:T(8,128)S(1)} %get-tuple-element.50), channel_id=1, source_target_pairs={{0,20},{4,16},{8,28},{12,24},{16,4},{20,0},{24,12},{28,8},{1,21},{... | collective-permute-start | bytes 24584 | tf_op jit(solution)/shard_map/ppermute | solution.py:566
  65.2 5.3 %collective-permute-start.13 = (f32[2,8,128]{2,1,0:T(8,128)S(1)}, f32[2,8,128]{2,1,0:T(8,128)S(1)}, u32[]{:S(2)}, u32[]{:S(2)}) collective-permute-start(f32[2,8,128]{2,1,0:T(8,128)S(1)} %get-tuple-element.51), channel_id=1, source_target_pairs={{0,12},{12,0},{16,28},{28,16},{1,13},{13,1},{17,29},{29,17},{2,14}... | collective-permute-start | bytes 24584 | tf_op jit(solution)/shard_map/ppermute | solution.py:566
  70.5 3.9 %collective-permute-start.11 = (f32[2,7,8,128]{3,2,1,0:T(8,128)S(1)}, f32[2,7,8,128]{3,2,1,0:T(8,128)S(1)}, u32[]{:S(2)}, u32[]{:S(2)}) collective-permute-start(f32[2,7,8,128]{3,2,1,0:T(8,128)S(1)} %get-tuple-element.49), channel_id=1, source_target_pairs={{0,16},{4,20},{8,24},{12,28},{16,0},{20,4},{24,8},{28,12},{1,17},{... | collective-permute-start | bytes 172040 | tf_op jit(solution)/shard_map/ppermute | solution.py:566
  74.5 11.5 %collective-permute-start.14 = (f32[59,8,128]{2,1,0:T(8,128)S(1)}, f32[59,8,128]{2,1,0:T(8,128)S(1)}, u32[]{:S(2)}, u32[]{:S(2)}) collective-permute-start(f32[59,8,128]{2,1,0:T(8,128)S(1)} %get-tuple-element.52), channel_id=1, source_target_pairs={{0,1},{1,0},{2,3},{3,2},{4,5},{5,4},{6,7},{7,6},{8,9},{9,8},{10,11... | collective-permute-start | bytes 725000 | tf_op jit(solution)/shard_map/ppermute | solution.py:573
  77.3 8.7 %collective-permute-start.15 = (f32[59,8,128]{2,1,0:T(8,128)S(1)}, f32[59,8,128]{2,1,0:T(8,128)S(1)}, u32[]{:S(2)}, u32[]{:S(2)}) collective-permute-start(f32[59,8,128]{2,1,0:T(8,128)S(1)} %get-tuple-element.53), channel_id=1, source_target_pairs={{1,2},{2,1},{5,6},{6,5},{9,10},{10,9},{13,14},{14,13},{17,18},{18,... | collective-permute-start | bytes 725000 | tf_op jit(solution)/shard_map/ppermute | solution.py:573
